TPU v7x, 256 devices: a whole 4x4x8 slice. The times are simulated.
256 devices in a mesh: dom: 256 (over y, x, z, core).
Axes of the slice: x: 4, y: 4, z: 8, core: 2. Of those that a mesh axis runs over, the one named last changes fastest.
Arguments:
- embeddings: float32 [131072, 400], P('dom'), may hold values from -1.8 to 1.8
- row_state: float32 [131072], P('dom'), may hold values from 0.01 to 1
- relations: float32 [2048, 400], P('dom'), may hold values from 0.5 to 1.5
- relation_state: float32 [2048], P('dom'), may hold values from 0.01 to 1
- partner_mask: int32 [1], replicated, may hold values from 1 to 255
- source_rows: int32 [786432], P('dom'), may hold values from 0 to 511
- relation_ids: int32 [786432], P('dom'), may hold values from 0 to 2047
- dest_rows: int32 [786432], P('dom'), may hold values from 0 to 511
- negative_rows: int32 [3072, 512], P('dom'), may hold values from 0 to 511
- edge_count: int32 [256], P('dom'), may hold values from 1 to 3072, 491520 in all
Outputs:
- new_embeddings: float32 [131072, 400], P('dom')
- new_row_state: float32 [131072], P('dom')
- new_relations: float32 [2048, 400], P('dom')
- new_relation_state: float32 [2048], P('dom')
Inputs may be any that keep to these rules, and one draw needn't show every extreme that they name: Device i trains the bucket of partition i with partition i XOR partner_mask[0]. `edge_count`: some bucket has all 3072 slots live.
All inputs are finite; a program needn't handle non-finite values. No bound on the sum of `edge_count` on one device may be relied on, other than what follows from the above.
Results may differ from a plain program's by a relative error of at most 0.0015.
Values may be sent and summed in bfloat16 or wider, within the bound.
No kernel may reach another device: no remote copies, remote signals or barrier semaphores. Data moves between devices by JAX's collectives and lax.ppermute only.
A program may use at most 128 MiB of HBM per device.

v0:
```python
import jax
import jax.numpy as jnp
from jax import lax
from jax.experimental import pallas as pl
from jax.experimental.pallas import tpu as pltpu
from jax.sharding import PartitionSpec as P

BF = jnp.bfloat16
F32 = jnp.float32
NT = (((1,), (1,)), ((), ()))
NN = (((1,), (0,)), ((), ()))

CORE_BITS, Z_BITS, XY_BITS = 1, 3, 4
Z_SHIFT, XY_SHIFT = CORE_BITS, CORE_BITS + Z_BITS


TILE = 256


def dot(a, b, dims):
    return lax.dot_general(a, b, dims, preferred_element_type=F32)


def one_hot(ids, tile):
    low = jnp.where(jnp.right_shift(ids, 8) == tile, jnp.bitwise_and(ids, TILE - 1), -1)
    low = jnp.broadcast_to(low.astype(F32), (TILE, ids.shape[1])).astype(BF)
    rows = lax.broadcasted_iota(jnp.int32, (TILE, ids.shape[1]), 0).astype(F32).astype(BF)
    return jnp.where(rows == low, jnp.ones((), BF), jnp.zeros((), BF))


def one_hots(ids, size):
    return jnp.concatenate([one_hot(ids, t) for t in range(size // TILE)], axis=0)


def identity(n):
    return (lax.broadcasted_iota(jnp.int32, (n, n), 0) == lax.broadcasted_iota(jnp.int32, (n, n), 1)).astype(BF)


def first_kernel(bt_ref, s_ref, n_ref, own_ref, sel_ref, times_ref):
    rows = bt_ref.shape[1]
    groups, glen = s_ref.shape
    negs = n_ref.shape[1]

    def group(g, carry):
        at = pl.ds(pl.multiple_of(g * glen, glen), glen)
        sel = one_hots(s_ref[pl.ds(g, 1), :], rows)
        sel_ref[:, at] = sel
        own_ref[:, at] = dot(bt_ref[...], sel, NN).astype(BF)
        hits = one_hots(n_ref[pl.ds(g, 1), :], rows)
        lanes = negs // 4
        four = (hits[:, :lanes] + hits[:, lanes:2 * lanes]) + (hits[:, 2 * lanes:3 * lanes] + hits[:, 3 * lanes:])
        times = jnp.sum(four.astype(F32), axis=1, keepdims=True) * (0.5 / negs)
        times_ref[pl.ds(g, 1)] = jnp.broadcast_to(times, (rows, 128)).astype(BF)[None]
        return carry

    lax.fori_loop(0, groups, group, 0)


def train_kernel(own_ref, times_ref, pt_ref, r0_ref, r1_ref, r_ref, d_ref, rall_ref,
                 part_ref, xo_ref, g0_ref, g1_ref,
                 rt, p, qa, wa, xr, sc0, rl0):
    width, rows = pt_ref.shape
    groups, glen = d_ref.shape
    half = r0_ref.shape[0]
    rels = 2 * half
    ident = identity(width)
    wide = 2 * TILE
    for k, ref in enumerate((r0_ref, r1_ref)):
        def turn(t, carry, k=k, ref=ref):
            at = pl.multiple_of(t * wide, wide)
            rt[:, pl.ds(k * half + at, wide)] = dot(ident, ref[pl.ds(at, wide), :], NT).astype(BF)
            return carry

        lax.fori_loop(0, half // wide, turn, 0)
    p[...] = (0.5 * dot(identity(rows), pt_ref[...], NT)).astype(BF)

    def span(g):
        return pl.ds(pl.multiple_of(g * glen, glen), glen)

    def forward(g, sc, rl):
        rel = dot(rt[...], one_hots(r_ref[pl.ds(g, 1), :], rels), NN).astype(BF)
        rl[...] = rel
        query = own_ref[:, span(g)] * rel
        qa[:, span(g)] = query
        sc[...] = dot(p[...], query, NN)

    def backward(g, sc, rl):
        score = sc[...]
        row = lax.broadcasted_iota(jnp.int32, (rows, glen), 0)
        hit = row == d_ref[pl.ds(g, 1), :]
        positive = jnp.sum(jnp.where(hit, score, 0.0), axis=0, keepdims=True)
        pos_grad = 0.5 * jnp.tanh(positive) - 0.5
        times = times_ref[pl.ds(g, 1)][0].astype(F32)
        times = jnp.concatenate([times, times], axis=1)
        weight = (jnp.tanh(score) + 1.0) * times
        weight = jnp.where(hit, weight + pos_grad, weight).astype(BF)
        wa[:, span(g)] = weight
        grad = dot(pt_ref[...], weight, NN).astype(BF)
        xo_ref[:, span(g)] = grad * rl[...]
        xr[:, span(g)] = grad * own_ref[:, span(g)]

    def group(g, carry):
        forward(g, sc0, rl0)
        backward(g, sc0, rl0)
        return carry

    lax.fori_loop(0, groups, group, 0)
    part_ref[...] = dot(qa[...], wa[...], NT).astype(BF)

    tiles = half // TILE

    def scatter(t, carry):
        out = dot(xr[...], one_hot(rall_ref[...], t), NT).T.astype(BF)
        at = pl.ds(pl.multiple_of(lax.rem(t, tiles) * TILE, TILE), TILE)

        @pl.when(t < tiles)
        def _():
            g0_ref[at, :] = out

        @pl.when(t >= tiles)
        def _():
            g1_ref[at, :] = out

        return carry

    lax.fori_loop(0, rels // TILE, scatter, 0)


def last_kernel(xo_ref, sel_ref, own_ref):
    own_ref[...] = dot(xo_ref[...], sel_ref[...], NT)


def swap(value, mask):
    pairs = [(source, source ^ mask) for source in range(lax.axis_size("dom"))]
    return lax.ppermute(value, "dom", pairs)


def groups_of(shift, bits):
    members = [m << shift for m in range(1 << bits)]
    rest = [b for b in range(lax.axis_size("dom")) if not b & (((1 << bits) - 1) << shift)]
    return [[b | m for m in members] for b in rest]


def exchange(blocks, shift, bits):
    return lax.all_to_all(blocks, "dom", 0, 0, axis_index_groups=groups_of(shift, bits))


def partner_step(mask, shift, bits, value):
    def branch(digit):
        return lambda moved: swap(moved, digit << shift) if digit else moved

    digit = jnp.bitwise_and(jnp.right_shift(mask, shift), (1 << bits) - 1)
    return lax.switch(digit, [branch(m) for m in range(1 << bits)], value)


def added(blocks):
    return jnp.sum(blocks.astype(F32), axis=0).astype(BF)


def local(
    embeddings,
    row_state,
    relations,
    relation_state,
    partner_mask,
    source_rows,
    relation_ids,
    dest_rows,
    negative_rows,
    edge_count,
):
    mask = partner_mask[0]
    groups = negative_rows.shape[0]
    rel_local, width = relations.shape
    rows = embeddings.shape[0]
    edges = source_rows.shape[0]
    me = lax.axis_index("dom")
    odd = jnp.bitwise_and(mask, 1) == 1
    z_size, xy_size = 1 << Z_BITS, 1 << XY_BITS
    half = z_size * xy_size * rel_local
    vm = pl.BlockSpec(memory_space=pltpu.VMEM)
    sh = jax.ShapeDtypeStruct

    own_t = embeddings.astype(BF).T
    rel_bf = relations.astype(BF)
    live = jnp.arange(edges, dtype=jnp.int32) < edge_count[0]
    own_edges, own_sel, times = pl.pallas_call(
        first_kernel,
        out_shape=(sh((width, edges), BF), sh((rows, edges), BF), sh((groups, rows, 128), BF)),
        in_specs=[vm] * 3, out_specs=(vm,) * 3, name="first",
    )(own_t, jnp.where(live, source_rows, -1).reshape(groups, -1), negative_rows)

    def spread(block, size):
        return jnp.broadcast_to(block[None], (size,) + block.shape)

    part_t = partner_step(mask, XY_SHIFT, XY_BITS, own_t)
    rel_z = exchange(spread(rel_bf, z_size), Z_SHIFT, Z_BITS).reshape(z_size * rel_local, width)
    rel_z, part_t = lax.optimization_barrier((rel_z, part_t))
    part_t = partner_step(mask, Z_SHIFT, Z_BITS, part_t)
    rel_here = exchange(spread(rel_z, xy_size), XY_SHIFT, XY_BITS)
    rel_here, part_t, own_edges = lax.optimization_barrier((rel_here, part_t, own_edges))
    rel_there = swap(rel_here, 1)
    part_t = jnp.where(odd, swap(part_t, 1), part_t)

    owner = relation_ids // rel_local
    core = jnp.bitwise_and(jnp.bitwise_xor(owner, me), 1)
    spot = core * half + jnp.right_shift(owner, CORE_BITS) * rel_local + relation_ids % rel_local

    part_grad, to_source, grad_here, grad_there = pl.pallas_call(
        train_kernel,
        out_shape=(sh((width, rows), BF), sh((width, edges), BF), sh((half, width), BF), sh((half, width), BF)),
        in_specs=[vm] * 8, out_specs=(vm,) * 4,
        scratch_shapes=[pltpu.VMEM((width, 2 * half), BF), pltpu.VMEM((rows, width), BF),
                        pltpu.VMEM((width, edges), BF), pltpu.VMEM((rows, edges), BF),
                        pltpu.VMEM((width, edges), BF),
                        pltpu.VMEM((rows, edges // groups), F32), pltpu.VMEM((width, edges // groups), BF)],
        name="train",
    )(own_edges, times, part_t, rel_here.reshape(half, width), rel_there.reshape(half, width),
      spot.reshape(groups, -1), dest_rows.reshape(groups, -1), spot.reshape(1, edges))

    by_z = (xy_size, z_size * rel_local, width)
    from_core = swap(grad_there.reshape(by_z), 1)
    part_core = swap(part_grad, 1)
    own_grad = pl.pallas_call(
        last_kernel, out_shape=sh((width, rows), F32), in_specs=[vm] * 2, out_specs=vm, name="last",
    )(to_source, own_sel)
    returned = jnp.where(odd, part_core, part_grad)
    grad_sum = (grad_here.reshape(by_z).astype(F32) + from_core.astype(F32)).astype(BF)
    grad_xy = added(exchange(grad_sum, XY_SHIFT, XY_BITS))
    returned = partner_step(mask, Z_SHIFT, Z_BITS, returned)
    grad_xy, returned, own_grad = lax.optimization_barrier((grad_xy, returned, own_grad))
    grad_z = exchange(grad_xy.reshape(z_size, rel_local, width), Z_SHIFT, Z_BITS)
    returned = partner_step(mask, XY_SHIFT, XY_BITS, returned)

    grad = (own_grad + returned.astype(F32)).T
    new_row_state = row_state + jnp.mean(grad * grad, axis=1)
    new_embeddings = embeddings - 0.1 * grad / jnp.sqrt(new_row_state)[:, None]
    rel_total = jnp.sum(grad_z.astype(F32), axis=0)
    new_relation_state = relation_state + jnp.mean(rel_total * rel_total, axis=1)
    new_relations = relations - 0.1 * rel_total / jnp.sqrt(new_relation_state)[:, None]
    return (new_embeddings, new_row_state, new_relations, new_relation_state)


def solution(mesh):
    in_specs = (
        P("dom", None),
        P("dom"),
        P("dom", None),
        P("dom"),
        P(),
        P("dom"),
        P("dom"),
        P("dom"),
        P("dom", None),
        P("dom"),
    )
    out_specs = (P("dom", None), P("dom"), P("dom", None), P("dom"))
    return jax.shard_map(local, mesh=mesh, in_specs=in_specs, out_specs=out_specs, check_vma=False)
```

profile of v0, /device:TPU:2, one launch (start us, length us, event | category | flops | bytes accessed | tf_op | source)
XLA Modules:
  0.0 177.9 jit_solution(4345618859830113258)
XLA Ops:
  0.6 0.7 convert_element_type.60
  1.4 0.6 broadcast_in_dim.8
  2.0 8.5 %all-to-all-start = ((bf16[8,8,400]{2,1,0:T(8,128)(2,1)}), bf16[8,8,400]{2,1,0:T(8,128)(2,1)S(1)}, u32[]{:S(2)}, u32[]{:S(2)}) async-start(bf16[8,8,400]{2,1,0:T(8,128)(2,1)} %broadcast_in_dim.8), calls=%async_computation | async-start | bytes 131072 | tf_op jit(solution)/shard_map/all_to_all | solution.py:145
  10.5 1.2 convert_bitcast_fusion.bt_ref
  12.3 15.1 %conditional.4 = (bf16[400,512]{1,0:T(8,128)(2,1)}) conditional(s32[]{:T(128)} %bitcast.1, bf16[400,512]{1,0:T(8,128)(2,1)S(1)} %convert_bitcast_fusion.bt_ref, bf16[400,512]{1,0:T(8,128)(2,1)S(1)} %convert_bitcast_fusion.bt_ref, bf16[400,512]{1,0:T(8,128)(2,1)S(1)} %convert_bitcast_fusion.bt_ref, ...), branch_computations={%region_0.1_spmd, %region_1.2_spmd, %region_2.3_spmd, %region_3.4_... | conditional | bytes 1638448 | solution.py:153
  12.4 4.8 %collective-permute-start.9 = (bf16[400,512]{1,0:T(8,128)(2,1)S(1)}, bf16[400,512]{1,0:T(8,128)(2,1)}, u32[]{:S(2)}, u32[]{:S(2)}) collective-permute-start(bf16[400,512]{1,0:T(8,128)(2,1)S(1)} %param.10), channel_id=1, source_target_pairs={{0,160},{1,161},{2,162},{3,163},{4,164},{5,165},{6,166},{7,167},{8... | collective-permute-start | bytes 1228808 | tf_op jit(solution)/shard_map/cond/branch_10_fun/ppermute | solution.py:135
  17.2 10.2 %collective-permute-done.9 = bf16[400,512]{1,0:T(8,128)(2,1)} collective-permute-done((bf16[400,512]{1,0:T(8,128)(2,1)S(1)}, bf16[400,512]{1,0:T(8,128)(2,1)}, u32[]{:S(2)}, u32[]{:S(2)}) %collective-permute-start.9) | collective-permute-done | bytes 409632 | tf_op jit(solution)/shard_map/cond/branch_10_fun/ppermute | solution.py:135
  27.4 1.1 broadcast_in_dim.9
  28.5 7.5 %all-to-all-start.1 = ((bf16[16,64,400]{2,1,0:T(8,128)(2,1)}), bf16[16,64,400]{2,1,0:T(8,128)(2,1)S(1)}, u32[]{:S(2)}, u32[]{:S(2)}) async-start(bf16[16,64,400]{2,1,0:T(8,128)(2,1)} %broadcast_in_dim.9), calls=%async_computation.1 | async-start | bytes 2097152 | tf_op jit(solution)/shard_map/all_to_all | solution.py:145
  37.2 7.1 %first.1 = (bf16[400,3072]{1,0:T(8,128)(2,1)}, bf16[512,3072]{1,0:T(8,128)(2,1)}, bf16[12,512,128]{2,1,0:T(8,128)(2,1)}) custom-call(bf16[400,512]{1,0:T(8,128)(2,1)S(1)} %convert_bitcast_fusion.bt_ref, s32[12,256]{1,0:T(8,128)} %reshape.61.s_ref, s32[12,512]{1,0:T(8,128)} %n_ref.1), custom_call_target="tpu_custom_call" | custom-call | tf_op jit(solution)/shard_map/first/pallas_call | solution.py:187
  44.4 20.1 %conditional.5 = (bf16[400,512]{1,0:T(8,128)(2,1)}) conditional(s32[]{:T(128)} %bitcast.3, bf16[400,512]{1,0:T(8,128)(2,1)} %get-tuple-element.144, bf16[400,512]{1,0:T(8,128)(2,1)} %get-tuple-element.144, bf16[400,512]{1,0:T(8,128)(2,1)} %get-tuple-element.144, bf16[400,512]{1,0:T(8,128)(2,1)} %get-tuple-element.144, ...), branch_computations={%region_16.17_spmd, %region_17.18_spmd, %region_18.19_spmd, %regio... | conditional | bytes 2457648 | solution.py:153
  44.4 2.6 %collective-permute-start.16 = (bf16[400,512]{1,0:T(8,128)(2,1)}, bf16[400,512]{1,0:T(8,128)(2,1)S(1)}, u32[]{:S(2)}, u32[]{:S(2)}) collective-permute-start(bf16[400,512]{1,0:T(8,128)(2,1)} %param.18), channel_id=1, source_target_pairs={{0,4},{1,5},{2,6},{3,7},{4,0},{5,1},{6,2},{7,3},{8,12},{9,13},{10,... | collective-permute-start | bytes 1228808 | tf_op jit(solution)/shard_map/cond/branch_2_fun/ppermute | solution.py:135
  47.0 16.8 %collective-permute-done.16 = bf16[400,512]{1,0:T(8,128)(2,1)S(1)} collective-permute-done((bf16[400,512]{1,0:T(8,128)(2,1)}, bf16[400,512]{1,0:T(8,128)(2,1)S(1)}, u32[]{:S(2)}, u32[]{:S(2)}) %collective-permute-start.16) | collective-permute-done | bytes 409632 | tf_op jit(solution)/shard_map/cond/branch_2_fun/ppermute | solution.py:135
  63.8 0.7 copy.32
  66.3 1.5 collective-permute-done.44
  67.8 1.8 %broadcast_select_fusion.1.pt_ref = bf16[400,512]{1,0:T(8,128)(2,1)} fusion(bf16[400,512]{1,0:T(8,128)(2,1)S(1)} %collective-permute-done.44, bf16[400,512]{1,0:T(8,128)(2,1)} %get-tuple-element.145, pred[]{:T(512)} %bitcast.5), kind=kLoop, calls=%fused_computation.7 | loop fusion | flops 204800 | bytes 1228801 | tf_op jit(solution)/shard_map/jit(_where)/select_n | solution.py:203
  69.6 1.0 copy-done.3
  70.7 37.2 %train.1 = (bf16[400,512]{1,0:T(8,128)(2,1)}, bf16[400,3072]{1,0:T(8,128)(2,1)}, bf16[1024,400]{1,0:T(8,128)(2,1)}, bf16[1024,400]{1,0:T(8,128)(2,1)}) custom-call(bf16[400,3072]{1,0:T(8,128)(2,1)} %get-tuple-element.128.own_ref, bf16[12,512,128]{2,1,0:T(8,128)(2,1)} %get-tuple-element.129.times_ref, bf16[400,512]{1,0:T(8,128)(2,1)} %broadcast_select_fusion.1.pt_ref, ...), custom_call_target="tpu_custom_call" | custom-call | tf_op jit(solution)/shard_map/train/pallas_call | solution.py:209
  108.0 2.7 %collective-permute-done.46 = bf16[16,64,400]{2,1,0:T(8,128)(2,1)S(1)} collective-permute-done((bf16[16,64,400]{2,1,0:T(8,128)(2,1)}, bf16[16,64,400]{2,1,0:T(8,128)(2,1)S(1)}, u32[]{:S(2)}, u32[]{:S(2)}) %collective-permute-start.46) | collective-permute-done | bytes 819232 | tf_op jit(solution)/shard_map/ppermute | solution.py:135
  110.7 2.6 %fusion = bf16[16,64,400]{2,1,0:T(8,128)(2,1)} fusion(bf16[16,64,400]{2,1,0:T(8,128)(2,1)} %bitcast.18, bf16[16,64,400]{2,1,0:T(8,128)(2,1)S(1)} %collective-permute-done.46), kind=kLoop, calls=%fused_computation.1 | loop fusion | flops 1638400 | bytes 2457600 | tf_op jit(solution)/shard_map/convert_element_type | solution.py:228
  113.3 7.2 %all-to-all-start.2 = ((bf16[16,64,400]{2,1,0:T(8,128)(2,1)}), bf16[16,64,400]{2,1,0:T(8,128)(2,1)S(1)}, u32[]{:S(2)}, u32[]{:S(2)}) async-start(bf16[16,64,400]{2,1,0:T(8,128)(2,1)} %fusion), calls=%async_computation.2 | async-start | bytes 2097152 | tf_op jit(solution)/shard_map/all_to_all | solution.py:145
  120.6 5.0 %last.1 = f32[400,512]{1,0:T(8,128)} custom-call(bf16[400,3072]{1,0:T(8,128)(2,1)} %get-tuple-element.135.xo_ref, bf16[512,3072]{1,0:T(8,128)(2,1)} %get-tuple-element.136.sel_ref), custom_call_target="tpu_custom_call" | custom-call | tf_op jit(solution)/shard_map/last/pallas_call | solution.py:224
  125.7 21.7 %conditional.6 = (bf16[400,512]{1,0:T(8,128)(2,1)S(1)}) conditional(s32[]{:T(128)} %bitcast.3, bf16[400,512]{1,0:T(8,128)(2,1)S(1)} %broadcast_select_fusion, bf16[400,512]{1,0:T(8,128)(2,1)S(1)} %broadcast_select_fusion, bf16[400,512]{1,0:T(8,128)(2,1)S(1)} %broadcast_select_fusion, ...), branch_computations={%region_25.26_spmd, %region_26.27_spmd, %region_27.28_spmd, %regio... | conditional | bytes 2457648 | solution.py:153
  125.8 21.5 %collective-permute-done.23 = bf16[400,512]{1,0:T(8,128)(2,1)S(1)} collective-permute-done((bf16[400,512]{1,0:T(8,128)(2,1)S(1)}, bf16[400,512]{1,0:T(8,128)(2,1)S(1)}, u32[]{:S(2)}, u32[]{:S(2)}) %collective-permute-start.23) | collective-permute-done | bytes 409632 | tf_op jit(solution)/shard_map/cond/branch_2_fun/ppermute | solution.py:135
  147.4 0.8 reduce_sum.39
  148.2 15.0 %conditional.7 = (bf16[400,512]{1,0:T(8,128)(2,1)S(1)}) conditional(s32[]{:T(128)} %bitcast.1, bf16[400,512]{1,0:T(8,128)(2,1)S(1)} %get-tuple-element.146, bf16[400,512]{1,0:T(8,128)(2,1)S(1)} %get-tuple-element.146, bf16[400,512]{1,0:T(8,128)(2,1)S(1)} %get-tuple-element.146, ...), branch_computations={%region_33.34_spmd, %region_34.35_spmd, %region_35.36_spmd, %regio... | conditional | bytes 2457648 | solution.py:153
  148.2 4.5 %collective-permute-start.38 = (bf16[400,512]{1,0:T(8,128)(2,1)S(1)}, bf16[400,512]{1,0:T(8,128)(2,1)S(1)}, u32[]{:S(2)}, u32[]{:S(2)}) collective-permute-start(bf16[400,512]{1,0:T(8,128)(2,1)S(1)} %param.42), channel_id=1, source_target_pairs={{0,160},{1,161},{2,162},{3,163},{4,164},{5,165},{6,166},{7,167},{8... | collective-permute-start | bytes 1228808 | tf_op jit(solution)/shard_map/cond/branch_10_fun/ppermute | solution.py:135
  152.7 10.4 %collective-permute-done.38 = bf16[400,512]{1,0:T(8,128)(2,1)S(1)} collective-permute-done((bf16[400,512]{1,0:T(8,128)(2,1)S(1)}, bf16[400,512]{1,0:T(8,128)(2,1)S(1)}, u32[]{:S(2)}, u32[]{:S(2)}) %collective-permute-start.38) | collective-permute-done | bytes 409632 | tf_op jit(solution)/shard_map/cond/branch_10_fun/ppermute | solution.py:135
  163.1 5.0 %all-to-all-start.3 = ((bf16[8,8,400]{2,1,0:T(8,128)(2,1)}), bf16[8,8,400]{2,1,0:T(8,128)(2,1)S(1)}, u32[]{:S(2)}, u32[]{:S(2)}) async-start(bf16[8,8,400]{2,1,0:T(8,128)(2,1)} %bitcast.12), calls=%async_computation.3 | async-start | bytes 131072 | tf_op jit(solution)/shard_map/all_to_all | solution.py:145
  168.9 1.1 bitcast_subtract_fusion
  170.1 6.5 %all-to-all-done.3 = bf16[8,8,400]{2,1,0:T(8,128)(2,1)S(1)} async-done(((bf16[8,8,400]{2,1,0:T(8,128)(2,1)}), bf16[8,8,400]{2,1,0:T(8,128)(2,1)S(1)}, u32[]{:S(2)}, u32[]{:S(2)}) %all-to-all-start.3) | async-done | bytes 51232 | tf_op jit(solution)/shard_map/all_to_all | solution.py:145
  177.2 0.7 divide_subtract_fusion
  (46 shorter events, 4.2 us)
Async XLA Ops:
  2.0 25.4 %all-to-all-start = ((bf16[8,8,400]{2,1,0:T(8,128)(2,1)}), bf16[8,8,400]{2,1,0:T(8,128)(2,1)S(1)}, u32[]{:S(2)}, u32[]{:S(2)}) async-start(bf16[8,8,400]{2,1,0:T(8,128)(2,1)} %broadcast_in_dim.8), calls=%async_computation | async-start | bytes 131072 | tf_op jit(solution)/shard_map/all_to_all | solution.py:145
  11.7 25.0 %copy-start.8 = (s32[3072]{0:T(1024)S(1)}, s32[3072]{0:T(1024)}, u32[]{:S(2)}) copy-start(s32[3072]{0:T(1024)} %param.63) | copy-start | bytes 36868
  12.4 15.0 %collective-permute-start.9 = (bf16[400,512]{1,0:T(8,128)(2,1)S(1)}, bf16[400,512]{1,0:T(8,128)(2,1)}, u32[]{:S(2)}, u32[]{:S(2)}) collective-permute-start(bf16[400,512]{1,0:T(8,128)(2,1)S(1)} %param.10), channel_id=1, source_target_pairs={{0,160},{1,161},{2,162},{3,163},{4,164},{5,165},{6,166},{7,167},{8... | collective-permute-start | bytes 1228808 | tf_op jit(solution)/shard_map/cond/branch_10_fun/ppermute | solution.py:135
  28.5 36.1 %all-to-all-start.1 = ((bf16[16,64,400]{2,1,0:T(8,128)(2,1)}), bf16[16,64,400]{2,1,0:T(8,128)(2,1)S(1)}, u32[]{:S(2)}, u32[]{:S(2)}) async-start(bf16[16,64,400]{2,1,0:T(8,128)(2,1)} %broadcast_in_dim.9), calls=%async_computation.1 | async-start | bytes 2097152 | tf_op jit(solution)/shard_map/all_to_all | solution.py:145
  44.4 20.7 %copy-start.9 = (s32[3072]{0:T(1024)S(1)}, s32[3072]{0:T(1024)}, u32[]{:S(2)}) copy-start(s32[3072]{0:T(1024)} %param.64) | copy-start | bytes 36868
  44.4 21.3 %copy-start.7 = (s32[3072]{0:T(1024)S(1)}, s32[3072]{0:T(1024)}, u32[]{:S(2)}) copy-start(s32[3072]{0:T(1024)} %param.65) | copy-start | bytes 36868
  44.4 19.4 %collective-permute-start.16 = (bf16[400,512]{1,0:T(8,128)(2,1)}, bf16[400,512]{1,0:T(8,128)(2,1)S(1)}, u32[]{:S(2)}, u32[]{:S(2)}) collective-permute-start(bf16[400,512]{1,0:T(8,128)(2,1)} %param.18), channel_id=1, source_target_pairs={{0,4},{1,5},{2,6},{3,7},{4,0},{5,1},{6,2},{7,3},{8,12},{9,13},{10,... | collective-permute-start | bytes 1228808 | tf_op jit(solution)/shard_map/cond/branch_2_fun/ppermute | solution.py:135
  64.5 5.1 %copy-start.1 = (bf16[16,64,400]{2,1,0:T(8,128)(2,1)}, bf16[16,64,400]{2,1,0:T(8,128)(2,1)S(1)}, u32[]{:S(2)}) copy-start(bf16[16,64,400]{2,1,0:T(8,128)(2,1)S(1)} %all-to-all-done.1) | copy-start | bytes 2457604
  64.5 5.1 %collective-permute-start.45 = (bf16[16,64,400]{2,1,0:T(8,128)(2,1)S(1)}, bf16[16,64,400]{2,1,0:T(8,128)(2,1)S(1)}, u32[]{:S(2)}, u32[]{:S(2)}) collective-permute-start(bf16[16,64,400]{2,1,0:T(8,128)(2,1)S(1)} %all-to-all-done.1), channel_id=1, source_target_pairs={{0,1},{1,0},{2,3},{3,2},{4,5},{5,4},{6,7},{7,6},{8,9},{9,8},{10,11... | collective-permute-start | bytes 2457608 | tf_op jit(solution)/shard_map/ppermute | solution.py:135
  64.5 3.2 %collective-permute-start.44 = (bf16[400,512]{1,0:T(8,128)(2,1)}, bf16[400,512]{1,0:T(8,128)(2,1)S(1)}, u32[]{:S(2)}, u32[]{:S(2)}) collective-permute-start(bf16[400,512]{1,0:T(8,128)(2,1)} %get-tuple-element.145), channel_id=1, source_target_pairs={{0,1},{1,0},{2,3},{3,2},{4,5},{5,4},{6,7},{7,6},{8,9},{9,8},{10,11... | collective-permute-start | bytes 1228808 | tf_op jit(solution)/shard_map/ppermute | solution.py:135
  65.1 4.5 %copy-start.5 = (s32[3072]{0:T(1024)}, s32[3072]{0:T(1024)S(1)}, u32[]{:S(2)}) copy-start(s32[3072]{0:T(1024)S(1)} %fusion.1) | copy-start | bytes 36868
  69.6 1.1 copy-start.3
  107.9 2.9 %collective-permute-start.46 = (bf16[16,64,400]{2,1,0:T(8,128)(2,1)}, bf16[16,64,400]{2,1,0:T(8,128)(2,1)S(1)}, u32[]{:S(2)}, u32[]{:S(2)}) collective-permute-start(bf16[16,64,400]{2,1,0:T(8,128)(2,1)} %bitcast.22), channel_id=1, source_target_pairs={{0,1},{1,0},{2,3},{3,2},{4,5},{5,4},{6,7},{7,6},{8,9},{9,8},{10,11... | collective-permute-start | bytes 2457608 | tf_op jit(solution)/shard_map/ppermute | solution.py:135
  110.7 9.8 %copy-start.4 = (bf16[400,512]{1,0:T(8,128)(2,1)S(1)}, bf16[400,512]{1,0:T(8,128)(2,1)}, u32[]{:S(2)}) copy-start(bf16[400,512]{1,0:T(8,128)(2,1)} %get-tuple-element.134) | copy-start | bytes 1228804
  113.3 34.1 %all-to-all-start.2 = ((bf16[16,64,400]{2,1,0:T(8,128)(2,1)}), bf16[16,64,400]{2,1,0:T(8,128)(2,1)S(1)}, u32[]{:S(2)}, u32[]{:S(2)}) async-start(bf16[16,64,400]{2,1,0:T(8,128)(2,1)} %fusion), calls=%async_computation.2 | async-start | bytes 2097152 | tf_op jit(solution)/shard_map/all_to_all | solution.py:145
  120.5 5.1 %collective-permute-start.47 = (bf16[400,512]{1,0:T(8,128)(2,1)S(1)}, bf16[400,512]{1,0:T(8,128)(2,1)S(1)}, u32[]{:S(2)}, u32[]{:S(2)}) collective-permute-start(bf16[400,512]{1,0:T(8,128)(2,1)S(1)} %copy-done.4), channel_id=1, source_target_pairs={{0,1},{1,0},{2,3},{3,2},{4,5},{5,4},{6,7},{7,6},{8,9},{9,8},{10,11... | collective-permute-start | bytes 1228808 | tf_op jit(solution)/shard_map/ppermute | solution.py:135
  125.7 21.6 %collective-permute-start.23 = (bf16[400,512]{1,0:T(8,128)(2,1)S(1)}, bf16[400,512]{1,0:T(8,128)(2,1)S(1)}, u32[]{:S(2)}, u32[]{:S(2)}) collective-permute-start(bf16[400,512]{1,0:T(8,128)(2,1)S(1)} %param.26), channel_id=1, source_target_pairs={{0,4},{1,5},{2,6},{3,7},{4,0},{5,1},{6,2},{7,3},{8,12},{9,13},{10,... | collective-permute-start | bytes 1228808 | tf_op jit(solution)/shard_map/cond/branch_2_fun/ppermute | solution.py:135
  148.2 20.0 %copy-start = (f32[400,512]{1,0:T(8,128)S(1)}, f32[400,512]{1,0:T(8,128)}, u32[]{:S(2)}) copy-start(f32[400,512]{1,0:T(8,128)} %last.1) | copy-start | bytes 2457604
  148.2 20.2 %copy-start.10 = (f32[512]{0:T(512)S(1)}, f32[512]{0:T(512)}, u32[]{:S(2)}) copy-start(f32[512]{0:T(512)} %param.59) | copy-start | bytes 6148
  148.2 20.8 %copy-start.2 = (f32[512,400]{0,1:T(8,128)S(1)}, f32[512,400]{0,1:T(8,128)}, u32[]{:S(2)}) copy-start(f32[512,400]{0,1:T(8,128)} %param.58) | copy-start | bytes 2457604
  148.2 14.9 %collective-permute-start.38 = (bf16[400,512]{1,0:T(8,128)(2,1)S(1)}, bf16[400,512]{1,0:T(8,128)(2,1)S(1)}, u32[]{:S(2)}, u32[]{:S(2)}) collective-permute-start(bf16[400,512]{1,0:T(8,128)(2,1)S(1)} %param.42), channel_id=1, source_target_pairs={{0,160},{1,161},{2,162},{3,163},{4,164},{5,165},{6,166},{7,167},{8... | collective-permute-start | bytes 1228808 | tf_op jit(solution)/shard_map/cond/branch_10_fun/ppermute | solution.py:135
  163.1 13.4 %all-to-all-start.3 = ((bf16[8,8,400]{2,1,0:T(8,128)(2,1)}), bf16[8,8,400]{2,1,0:T(8,128)(2,1)S(1)}, u32[]{:S(2)}, u32[]{:S(2)}) async-start(bf16[8,8,400]{2,1,0:T(8,128)(2,1)} %bitcast.12), calls=%async_computation.3 | async-start | bytes 131072 | tf_op jit(solution)/shard_map/all_to_all | solution.py:145
  168.2 8.5 %copy-start.11 = (f32[8]{0:T(128)S(1)}, f32[8]{0:T(128)}, u32[]{:S(2)}) copy-start(f32[8]{0:T(128)} %param.61) | copy-start | bytes 100
  168.2 9.0 %copy-start.6 = (f32[8,400]{1,0:T(8,128)S(1)}, f32[8,400]{1,0:T(8,128)}, u32[]{:S(2)}) copy-start(f32[8,400]{1,0:T(8,128)} %param.60) | copy-start | bytes 38404
where the time goes:
time: 179 us; the launch traced here: 178 us
  waiting for transfers between devices  69.6 us (39%)
  Pallas kernels  49.3 us (28%)
  starting transfers between devices  41 us (23%)
  other arithmetic  10.4 us (6%)
  local copies, waits for them, and re-layouts  5.43 us (3%)
  between operations  2.09 us (1%)
    ppermute x8, waiting for transfers between devices, swap(): return lax.ppermute(value, 'dom', pairs)  63.1 us
    pallas_call x1, Pallas kernels, local(): pl.pallas_call(train_kernel, out_shape=(sh((width, rows), BF), sh((width,...  37.2 us
    all_to_all x4, starting transfers between devices, exchange(): lax.all_to_all(blocks, 'dom', 0, 0, axis_index_groups=groups_of(shift, bi...  28.2 us
    ppermute x8, starting transfers between devices, swap(): return lax.ppermute(value, 'dom', pairs)  12.8 us
    pallas_call x1, Pallas kernels, local(): pl.pallas_call(first_kernel, out_shape=(sh((width, edges), BF), sh((rows,...  7.13 us
    all_to_all x4, waiting for transfers between devices, exchange(): lax.all_to_all(blocks, 'dom', 0, 0, axis_index_groups=groups_of(shift, bi...  6.5 us
    pallas_call x1, Pallas kernels, local(): pl.pallas_call(last_kernel, out_shape=sh((width, rows), F32), in_specs=[v...  4.99 us
  transfers between devices with their start and end apart: 12, of which 7 were waited for; matrix products, arithmetic and copies ran while one was open for 4% of the time, Pallas kernels for 7%

commit v1 on v0

--- a/solution.py
+++ b/solution.py
@@ -36,35 +36,19 @@
     return (lax.broadcasted_iota(jnp.int32, (n, n), 0) == lax.broadcasted_iota(jnp.int32, (n, n), 1)).astype(BF)
 
 
-def first_kernel(bt_ref, s_ref, n_ref, own_ref, sel_ref, times_ref):
-    rows = bt_ref.shape[1]
-    groups, glen = s_ref.shape
-    negs = n_ref.shape[1]
-
-    def group(g, carry):
-        at = pl.ds(pl.multiple_of(g * glen, glen), glen)
-        sel = one_hots(s_ref[pl.ds(g, 1), :], rows)
-        sel_ref[:, at] = sel
-        own_ref[:, at] = dot(bt_ref[...], sel, NN).astype(BF)
-        hits = one_hots(n_ref[pl.ds(g, 1), :], rows)
-        lanes = negs // 4
-        four = (hits[:, :lanes] + hits[:, lanes:2 * lanes]) + (hits[:, 2 * lanes:3 * lanes] + hits[:, 3 * lanes:])
-        times = jnp.sum(four.astype(F32), axis=1, keepdims=True) * (0.5 / negs)
-        times_ref[pl.ds(g, 1)] = jnp.broadcast_to(times, (rows, 128)).astype(BF)[None]
-        return carry
-
-    lax.fori_loop(0, groups, group, 0)
-
-
-def train_kernel(own_ref, times_ref, pt_ref, r0_ref, r1_ref, r_ref, d_ref, rall_ref,
+def train_kernel(odd_ref, bt_ref, pa_ref, pb_ref, r0_ref, r1_ref, s_ref, r_ref, d_ref, n_ref, rall_ref,
                  part_ref, xo_ref, g0_ref, g1_ref,
-                 rt, p, qa, wa, xr, sc0, rl0):
-    width, rows = pt_ref.shape
-    groups, glen = d_ref.shape
+                 rt, pt, p, own, rl, qa, wa, xr, times_all, sc0, sc1):
+    width, rows = pa_ref.shape
+    groups, negs = n_ref.shape
+    edges = rall_ref.shape[1]
+    glen = edges // groups
     half = r0_ref.shape[0]
     rels = 2 * half
     ident = identity(width)
-    wide = 2 * TILE
+    wide = TILE
+    pt[...] = jnp.where(odd_ref[0] == 1, pb_ref[...], pa_ref[...])
+    p[...] = (0.5 * pt[...].astype(F32)).T.astype(BF)
     for k, ref in enumerate((r0_ref, r1_ref)):
         def turn(t, carry, k=k, ref=ref):
             at = pl.multiple_of(t * wide, wide)
@@ -72,41 +56,61 @@
             return carry
 
         lax.fori_loop(0, half // wide, turn, 0)
-    p[...] = (0.5 * dot(identity(rows), pt_ref[...], NT)).astype(BF)
 
     def span(g):
         return pl.ds(pl.multiple_of(g * glen, glen), glen)
 
-    def forward(g, sc, rl):
-        rel = dot(rt[...], one_hots(r_ref[pl.ds(g, 1), :], rels), NN).astype(BF)
-        rl[...] = rel
-        query = own_ref[:, span(g)] * rel
+    def ids(ref, g):
+        lines = glen // 128
+        got = ref[pl.ds(g * lines, lines), :]
+        return jnp.concatenate([got[i:i + 1] for i in range(lines)], axis=1)
+
+    def forward(g, sc):
+        mine = dot(bt_ref[...], one_hots(ids(s_ref, g), rows), NN).astype(BF)
+        own[:, span(g)] = mine
+        rel = dot(rt[...], one_hots(ids(r_ref, g), rels), NN).astype(BF)
+        rl[:, span(g)] = rel
+        query = mine * rel
         qa[:, span(g)] = query
         sc[...] = dot(p[...], query, NN)
-
-    def backward(g, sc, rl):
+        hits = one_hots(n_ref[pl.ds(g, 1), :], rows)
+        lanes = negs // 4
+        four = (hits[:, :lanes] + hits[:, lanes:2 * lanes]) + (hits[:, 2 * lanes:3 * lanes] + hits[:, 3 * lanes:])
+        times = jnp.sum(four.astype(F32), axis=1, keepdims=True) * (0.5 / negs)
+        times_all[pl.ds(g, 1)] = jnp.broadcast_to(times, (rows, 128)).astype(BF)[None]
+
+    def backward(g, sc):
         score = sc[...]
         row = lax.broadcasted_iota(jnp.int32, (rows, glen), 0)
-        hit = row == d_ref[pl.ds(g, 1), :]
+        hit = row == ids(d_ref, g)
         positive = jnp.sum(jnp.where(hit, score, 0.0), axis=0, keepdims=True)
         pos_grad = 0.5 * jnp.tanh(positive) - 0.5
-        times = times_ref[pl.ds(g, 1)][0].astype(F32)
+        times = times_all[pl.ds(g, 1)][0].astype(F32)
         times = jnp.concatenate([times, times], axis=1)
         weight = (jnp.tanh(score) + 1.0) * times
         weight = jnp.where(hit, weight + pos_grad, weight).astype(BF)
         wa[:, span(g)] = weight
-        grad = dot(pt_ref[...], weight, NN).astype(BF)
-        xo_ref[:, span(g)] = grad * rl[...]
-        xr[:, span(g)] = grad * own_ref[:, span(g)]
-
-    def group(g, carry):
-        forward(g, sc0, rl0)
-        backward(g, sc0, rl0)
-        return carry
-
-    lax.fori_loop(0, groups, group, 0)
-    part_ref[...] = dot(qa[...], wa[...], NT).astype(BF)
-
+        grad = dot(pt[...], weight, NN).astype(BF)
+        xo_ref[:, span(g)] = grad * rl[:, span(g)]
+        xr[:, span(g)] = grad * own[:, span(g)]
+
+    forward(0, sc0)
+
+    def pair(i, carry):
+        forward(2 * i + 1, sc1)
+        backward(2 * i, sc0)
+        forward(jnp.minimum(2 * i + 2, groups - 1), sc0)
+        backward(2 * i + 1, sc1)
+        return carry
+
+    lax.fori_loop(0, groups // 2, pair, 0)
+
+    def onto_rows(t, carry):
+        at = pl.ds(pl.multiple_of(t * TILE, TILE), TILE)
+        part_ref[:, at] = dot(qa[...], wa[at, :], NT).astype(BF)
+        return carry
+
+    lax.fori_loop(0, rows // TILE, onto_rows, 0)
     tiles = half // TILE
 
     def scatter(t, carry):
@@ -126,8 +130,12 @@
     lax.fori_loop(0, rels // TILE, scatter, 0)
 
 
-def last_kernel(xo_ref, sel_ref, own_ref):
-    own_ref[...] = dot(xo_ref[...], sel_ref[...], NT)
+def last_kernel(xo_ref, sall_ref, own_ref):
+    def onto_rows(t, carry):
+        own_ref[:, pl.ds(pl.multiple_of(t * TILE, TILE), TILE)] = dot(xo_ref[...], one_hot(sall_ref[...], t), NT)
+        return carry
+
+    lax.fori_loop(0, own_ref.shape[1] // TILE, onto_rows, 0)
 
 
 def swap(value, mask):
@@ -183,12 +191,6 @@
 
     own_t = embeddings.astype(BF).T
     rel_bf = relations.astype(BF)
-    live = jnp.arange(edges, dtype=jnp.int32) < edge_count[0]
-    own_edges, own_sel, times = pl.pallas_call(
-        first_kernel,
-        out_shape=(sh((width, edges), BF), sh((rows, edges), BF), sh((groups, rows, 128), BF)),
-        in_specs=[vm] * 3, out_specs=(vm,) * 3, name="first",
-    )(own_t, jnp.where(live, source_rows, -1).reshape(groups, -1), negative_rows)
 
     def spread(block, size):
         return jnp.broadcast_to(block[None], (size,) + block.shape)
@@ -198,32 +200,36 @@
     rel_z, part_t = lax.optimization_barrier((rel_z, part_t))
     part_t = partner_step(mask, Z_SHIFT, Z_BITS, part_t)
     rel_here = exchange(spread(rel_z, xy_size), XY_SHIFT, XY_BITS)
-    rel_here, part_t, own_edges = lax.optimization_barrier((rel_here, part_t, own_edges))
+    rel_here, part_t = lax.optimization_barrier((rel_here, part_t))
     rel_there = swap(rel_here, 1)
-    part_t = jnp.where(odd, swap(part_t, 1), part_t)
+    part_there = swap(part_t, 1)
 
     owner = relation_ids // rel_local
     core = jnp.bitwise_and(jnp.bitwise_xor(owner, me), 1)
     spot = core * half + jnp.right_shift(owner, CORE_BITS) * rel_local + relation_ids % rel_local
 
+    live_sources = jnp.where(jnp.arange(edges, dtype=jnp.int32) < edge_count[0], source_rows, -1)
+
     part_grad, to_source, grad_here, grad_there = pl.pallas_call(
         train_kernel,
         out_shape=(sh((width, rows), BF), sh((width, edges), BF), sh((half, width), BF), sh((half, width), BF)),
-        in_specs=[vm] * 8, out_specs=(vm,) * 4,
-        scratch_shapes=[pltpu.VMEM((width, 2 * half), BF), pltpu.VMEM((rows, width), BF),
-                        pltpu.VMEM((width, edges), BF), pltpu.VMEM((rows, edges), BF),
-                        pltpu.VMEM((width, edges), BF),
-                        pltpu.VMEM((rows, edges // groups), F32), pltpu.VMEM((width, edges // groups), BF)],
+        in_specs=[pl.BlockSpec(memory_space=pltpu.SMEM)] + [vm] * 10, out_specs=(vm,) * 4,
+        scratch_shapes=[pltpu.VMEM((width, 2 * half), BF), pltpu.VMEM((width, rows), BF), pltpu.VMEM((rows, width), BF),
+                        *[pltpu.VMEM((width, edges), BF)] * 3, pltpu.VMEM((rows, edges), BF), pltpu.VMEM((width, edges), BF),
+                        pltpu.VMEM((groups, rows, 128), BF),
+                        pltpu.VMEM((rows, edges // groups), F32), pltpu.VMEM((rows, edges // groups), F32)],
         name="train",
-    )(own_edges, times, part_t, rel_here.reshape(half, width), rel_there.reshape(half, width),
-      spot.reshape(groups, -1), dest_rows.reshape(groups, -1), spot.reshape(1, edges))
+    )(jnp.bitwise_and(partner_mask, 1), own_t, part_t, part_there,
+      rel_here.reshape(half, width), rel_there.reshape(half, width),
+      live_sources.reshape(-1, 128), spot.reshape(-1, 128), dest_rows.reshape(-1, 128), negative_rows,
+      spot.reshape(1, edges))
 
     by_z = (xy_size, z_size * rel_local, width)
     from_core = swap(grad_there.reshape(by_z), 1)
     part_core = swap(part_grad, 1)
     own_grad = pl.pallas_call(
         last_kernel, out_shape=sh((width, rows), F32), in_specs=[vm] * 2, out_specs=vm, name="last",
-    )(to_source, own_sel)
+    )(to_source, live_sources.reshape(1, edges))
     returned = jnp.where(odd, part_core, part_grad)
     grad_sum = (grad_here.reshape(by_z).astype(F32) + from_core.astype(F32)).astype(BF)
     grad_xy = added(exchange(grad_sum, XY_SHIFT, XY_BITS))

time: 179 us -> 158 us (0.88)
  Pallas kernels: 49.3 us -> 37 us
  waiting for transfers between devices: 69.6 us -> 61.9 us
    pallas_call x1 -> x0, Pallas kernels: 7.13 us -> none  [local(): pl.pallas_call(first_kernel, out_shape=(sh((width, edges), BF), sh((rows,...]
    all_to_all x4, waiting for transfers between devices: 6.5 us -> 0.01 us  [exchange(): lax.all_to_all(blocks, 'dom', 0, 0, axis_index_groups=groups_of(shift, bi...]
    pallas_call x1, Pallas kernels: 37.2 us -> 32.8 us  [local(): pl.pallas_call(train_kernel, out_shape=(sh((width, rows), BF), sh((width,...]
    reshape x3 -> x0, local copies, waits for them, and re-layouts: 1.82 us -> none  [the longest x1 0.61 us: local(): jnp.where(live, source_rows, -1).reshape(groups, -1)]
  transfers between devices with their start and end apart: 12 -> 12, of which waited for: 7 -> 6; matrix products, arithmetic and copies ran while one was open for 4% -> 4% of each run, Pallas kernels for 7% -> 3%
where the time goes in v1:
time: 158 us; the launch traced here: 157 us
  waiting for transfers between devices  61.9 us (39%)
  starting transfers between devices  40.9 us (26%)
  Pallas kernels  37 us (23%)
  other arithmetic  11 us (7%)
  local copies, waits for them, and re-layouts  3.81 us (2%)
  between operations  2.1 us (1%)
    ppermute x8, waiting for transfers between devices, swap(): return lax.ppermute(value, 'dom', pairs)  61.9 us
    pallas_call x1, Pallas kernels, local(): pl.pallas_call(train_kernel, out_shape=(sh((width, rows), BF), sh((width,...  32.8 us
    all_to_all x4, starting transfers between devices, exchange(): lax.all_to_all(blocks, 'dom', 0, 0, axis_index_groups=groups_of(shift, bi...  27.7 us
    ppermute x8, starting transfers between devices, swap(): return lax.ppermute(value, 'dom', pairs)  13.2 us
    pallas_call x1, Pallas kernels, local(): pl.pallas_call(last_kernel, out_shape=sh((width, rows), F32), in_specs=[v...  4.26 us
  transfers between devices with their start and end apart: 12, of which 6 were waited for; matrix products, arithmetic and copies ran while one was open for 4% of the time, Pallas kernels for 3%

profile of v1, /device:TPU:2, one launch (start us, length us, event | category | flops | bytes accessed | tf_op | source)
XLA Modules:
  0.0 157.1 jit_solution(9731188799196247818)
XLA Ops:
  0.6 0.7 convert_element_type.61
  1.4 0.6 broadcast_in_dim.7
  2.0 8.5 %all-to-all-start = ((bf16[8,8,400]{2,1,0:T(8,128)(2,1)}), bf16[8,8,400]{2,1,0:T(8,128)(2,1)S(1)}, u32[]{:S(2)}, u32[]{:S(2)}) async-start(bf16[8,8,400]{2,1,0:T(8,128)(2,1)} %broadcast_in_dim.7), calls=%async_computation | async-start | bytes 131072 | tf_op jit(solution)/shard_map/all_to_all | solution.py:153
  10.5 1.2 convert_bitcast_fusion.bt_ref
  12.3 15.1 %conditional.4 = (bf16[400,512]{1,0:T(8,128)(2,1)}) conditional(s32[]{:T(128)} %bitcast.2, bf16[400,512]{1,0:T(8,128)(2,1)S(1)} %convert_bitcast_fusion.bt_ref, bf16[400,512]{1,0:T(8,128)(2,1)S(1)} %convert_bitcast_fusion.bt_ref, bf16[400,512]{1,0:T(8,128)(2,1)S(1)} %convert_bitcast_fusion.bt_ref, ...), branch_computations={%region_0.0_spmd, %region_1.0_spmd, %region_2.0_spmd, %region_3.0_... | conditional | bytes 1638448 | solution.py:161
  12.3 4.8 %collective-permute-start.9 = (bf16[400,512]{1,0:T(8,128)(2,1)S(1)}, bf16[400,512]{1,0:T(8,128)(2,1)}, u32[]{:S(2)}, u32[]{:S(2)}) collective-permute-start(bf16[400,512]{1,0:T(8,128)(2,1)S(1)} %param.10), channel_id=1, source_target_pairs={{0,160},{1,161},{2,162},{3,163},{4,164},{5,165},{6,166},{7,167},{8... | collective-permute-start | bytes 1228808 | tf_op jit(solution)/shard_map/cond/branch_10_fun/ppermute | solution.py:143
  17.2 10.2 %collective-permute-done.9 = bf16[400,512]{1,0:T(8,128)(2,1)} collective-permute-done((bf16[400,512]{1,0:T(8,128)(2,1)S(1)}, bf16[400,512]{1,0:T(8,128)(2,1)}, u32[]{:S(2)}, u32[]{:S(2)}) %collective-permute-start.9) | collective-permute-done | bytes 409632 | tf_op jit(solution)/shard_map/cond/branch_10_fun/ppermute | solution.py:143
  27.4 1.1 broadcast_in_dim.8
  28.5 7.5 %all-to-all-start.1 = ((bf16[16,64,400]{2,1,0:T(8,128)(2,1)}), bf16[16,64,400]{2,1,0:T(8,128)(2,1)S(1)}, u32[]{:S(2)}, u32[]{:S(2)}) async-start(bf16[16,64,400]{2,1,0:T(8,128)(2,1)} %broadcast_in_dim.8), calls=%async_computation.1 | async-start | bytes 2097152 | tf_op jit(solution)/shard_map/all_to_all | solution.py:153
  36.0 20.3 %conditional.5 = (bf16[400,512]{1,0:T(8,128)(2,1)}) conditional(s32[]{:T(128)} %bitcast.3, bf16[400,512]{1,0:T(8,128)(2,1)} %get-tuple-element.136, bf16[400,512]{1,0:T(8,128)(2,1)} %get-tuple-element.136, bf16[400,512]{1,0:T(8,128)(2,1)} %get-tuple-element.136, bf16[400,512]{1,0:T(8,128)(2,1)} %get-tuple-element.136, ...), branch_computations={%region_16.0_spmd, %region_17.0_spmd, %region_18.0_spmd, %region_1... | conditional | bytes 2457648 | solution.py:161
  36.0 2.7 %collective-permute-start.16 = (bf16[400,512]{1,0:T(8,128)(2,1)}, bf16[400,512]{1,0:T(8,128)(2,1)S(1)}, u32[]{:S(2)}, u32[]{:S(2)}) collective-permute-start(bf16[400,512]{1,0:T(8,128)(2,1)} %param.18), channel_id=1, source_target_pairs={{0,4},{1,5},{2,6},{3,7},{4,0},{5,1},{6,2},{7,3},{8,12},{9,13},{10,... | collective-permute-start | bytes 1228808 | tf_op jit(solution)/shard_map/cond/branch_2_fun/ppermute | solution.py:143
  38.8 16.8 %collective-permute-done.16 = bf16[400,512]{1,0:T(8,128)(2,1)S(1)} collective-permute-done((bf16[400,512]{1,0:T(8,128)(2,1)}, bf16[400,512]{1,0:T(8,128)(2,1)S(1)}, u32[]{:S(2)}, u32[]{:S(2)}) %collective-permute-start.16) | collective-permute-done | bytes 409632 | tf_op jit(solution)/shard_map/cond/branch_2_fun/ppermute | solution.py:143
  55.5 0.8 copy.32
  57.0 0.6 fusion.1
  58.1 0.6 fusion.9.r_ref
  58.7 0.6 fusion.10.s_ref
  59.7 0.7 copy-done.5
  60.8 32.8 %train.1 = (bf16[400,512]{1,0:T(8,128)(2,1)}, bf16[400,3072]{1,0:T(8,128)(2,1)}, bf16[1024,400]{1,0:T(8,128)(2,1)}, bf16[1024,400]{1,0:T(8,128)(2,1)}) custom-call(s32[1]{0:T(128)S(6)} %and.29.odd_ref, bf16[400,512]{1,0:T(8,128)(2,1)S(1)} %convert_bitcast_fusion.bt_ref, bf16[400,512]{1,0:T(8,128)(2,1)} %get-tuple-element.137.pa_ref, ...), custom_call_target="tpu_custom_call" | custom-call | tf_op jit(solution)/shard_map/train/pallas_call | solution.py:213
  94.0 2.5 %collective-permute-done.46 = bf16[16,64,400]{2,1,0:T(8,128)(2,1)S(1)} collective-permute-done((bf16[16,64,400]{2,1,0:T(8,128)(2,1)}, bf16[16,64,400]{2,1,0:T(8,128)(2,1)S(1)}, u32[]{:S(2)}, u32[]{:S(2)}) %collective-permute-start.46) | collective-permute-done | bytes 819232 | tf_op jit(solution)/shard_map/ppermute | solution.py:143
  96.5 2.6 %fusion = bf16[16,64,400]{2,1,0:T(8,128)(2,1)} fusion(bf16[16,64,400]{2,1,0:T(8,128)(2,1)} %bitcast.25, bf16[16,64,400]{2,1,0:T(8,128)(2,1)S(1)} %collective-permute-done.46), kind=kLoop, calls=%fused_computation.1 | loop fusion | flops 1638400 | bytes 2457600 | tf_op jit(solution)/shard_map/convert_element_type | solution.py:234
  99.1 7.2 %all-to-all-start.2 = ((bf16[16,64,400]{2,1,0:T(8,128)(2,1)}), bf16[16,64,400]{2,1,0:T(8,128)(2,1)S(1)}, u32[]{:S(2)}, u32[]{:S(2)}) async-start(bf16[16,64,400]{2,1,0:T(8,128)(2,1)} %fusion), calls=%async_computation.2 | async-start | bytes 2097152 | tf_op jit(solution)/shard_map/all_to_all | solution.py:153
  106.4 0.6 fusion.4
  107.0 4.3 %last.1 = f32[400,512]{1,0:T(8,128)} custom-call(bf16[400,3072]{1,0:T(8,128)(2,1)} %get-tuple-element.128.xo_ref, s32[1,3072]{1,0:T(1,128)} %bitcast.29), custom_call_target="tpu_custom_call" | custom-call | tf_op jit(solution)/shard_map/last/pallas_call | solution.py:230
  111.3 21.9 %conditional.6 = (bf16[400,512]{1,0:T(8,128)(2,1)S(1)}) conditional(s32[]{:T(128)} %bitcast.3, bf16[400,512]{1,0:T(8,128)(2,1)S(1)} %broadcast_select_fusion, bf16[400,512]{1,0:T(8,128)(2,1)S(1)} %broadcast_select_fusion, bf16[400,512]{1,0:T(8,128)(2,1)S(1)} %broadcast_select_fusion, ...), branch_computations={%region_25.26_spmd, %region_26.27_spmd, %region_27.28_spmd, %regio... | conditional | bytes 2457648 | solution.py:161
  111.5 21.5 %collective-permute-done.23 = bf16[400,512]{1,0:T(8,128)(2,1)S(1)} collective-permute-done((bf16[400,512]{1,0:T(8,128)(2,1)S(1)}, bf16[400,512]{1,0:T(8,128)(2,1)S(1)}, u32[]{:S(2)}, u32[]{:S(2)}) %collective-permute-start.23) | collective-permute-done | bytes 409632 | tf_op jit(solution)/shard_map/cond/branch_2_fun/ppermute | solution.py:143
  133.3 0.8 reduce_sum.39
  134.1 4.6 %all-to-all-start.3 = ((bf16[8,8,400]{2,1,0:T(8,128)(2,1)}), bf16[8,8,400]{2,1,0:T(8,128)(2,1)S(1)}, u32[]{:S(2)}, u32[]{:S(2)}) async-start(bf16[8,8,400]{2,1,0:T(8,128)(2,1)} %bitcast.16), calls=%async_computation.3 | async-start | bytes 131072 | tf_op jit(solution)/shard_map/all_to_all | solution.py:153
  138.6 15.2 %conditional.7 = (bf16[400,512]{1,0:T(8,128)(2,1)S(1)}) conditional(s32[]{:T(128)} %bitcast.2, bf16[400,512]{1,0:T(8,128)(2,1)S(1)} %get-tuple-element.138, bf16[400,512]{1,0:T(8,128)(2,1)S(1)} %get-tuple-element.138, bf16[400,512]{1,0:T(8,128)(2,1)S(1)} %get-tuple-element.138, ...), branch_computations={%region_33.34_spmd, %region_34.35_spmd, %region_35.36_spmd, %regio... | conditional | bytes 2457648 | solution.py:161
  138.7 4.6 %collective-permute-start.38 = (bf16[400,512]{1,0:T(8,128)(2,1)S(1)}, bf16[400,512]{1,0:T(8,128)(2,1)S(1)}, u32[]{:S(2)}, u32[]{:S(2)}) collective-permute-start(bf16[400,512]{1,0:T(8,128)(2,1)S(1)} %param.42), channel_id=1, source_target_pairs={{0,160},{1,161},{2,162},{3,163},{4,164},{5,165},{6,166},{7,167},{8... | collective-permute-start | bytes 1228808 | tf_op jit(solution)/shard_map/cond/branch_10_fun/ppermute | solution.py:143
  143.3 10.6 %collective-permute-done.38 = bf16[400,512]{1,0:T(8,128)(2,1)S(1)} collective-permute-done((bf16[400,512]{1,0:T(8,128)(2,1)S(1)}, bf16[400,512]{1,0:T(8,128)(2,1)S(1)}, u32[]{:S(2)}, u32[]{:S(2)}) %collective-permute-start.38) | collective-permute-done | bytes 409632 | tf_op jit(solution)/shard_map/cond/branch_10_fun/ppermute | solution.py:143
  154.7 1.1 bitcast_subtract_fusion
  156.4 0.7 divide_subtract_fusion
  (41 shorter events, 3.3 us)
Async XLA Ops:
  2.0 25.4 %all-to-all-start = ((bf16[8,8,400]{2,1,0:T(8,128)(2,1)}), bf16[8,8,400]{2,1,0:T(8,128)(2,1)S(1)}, u32[]{:S(2)}, u32[]{:S(2)}) async-start(bf16[8,8,400]{2,1,0:T(8,128)(2,1)} %broadcast_in_dim.7), calls=%async_computation | async-start | bytes 131072 | tf_op jit(solution)/shard_map/all_to_all | solution.py:153
  12.3 15.0 %collective-permute-start.9 = (bf16[400,512]{1,0:T(8,128)(2,1)S(1)}, bf16[400,512]{1,0:T(8,128)(2,1)}, u32[]{:S(2)}, u32[]{:S(2)}) collective-permute-start(bf16[400,512]{1,0:T(8,128)(2,1)S(1)} %param.10), channel_id=1, source_target_pairs={{0,160},{1,161},{2,162},{3,163},{4,164},{5,165},{6,166},{7,167},{8... | collective-permute-start | bytes 1228808 | tf_op jit(solution)/shard_map/cond/branch_10_fun/ppermute | solution.py:143
  28.5 27.8 %all-to-all-start.1 = ((bf16[16,64,400]{2,1,0:T(8,128)(2,1)}), bf16[16,64,400]{2,1,0:T(8,128)(2,1)S(1)}, u32[]{:S(2)}, u32[]{:S(2)}) async-start(bf16[16,64,400]{2,1,0:T(8,128)(2,1)} %broadcast_in_dim.8), calls=%async_computation.1 | async-start | bytes 2097152 | tf_op jit(solution)/shard_map/all_to_all | solution.py:153
  36.0 21.0 %copy-start.7 = (s32[3072]{0:T(1024)S(1)}, s32[3072]{0:T(1024)}, u32[]{:S(2)}) copy-start(s32[3072]{0:T(1024)} %param.64) | copy-start | bytes 36868
  36.0 22.7 %copy-start.8 = (s32[3072]{0:T(1024)S(1)}, s32[3072]{0:T(1024)}, u32[]{:S(2)}) copy-start(s32[3072]{0:T(1024)} %param.63) | copy-start | bytes 36868
  36.0 19.5 %collective-permute-start.16 = (bf16[400,512]{1,0:T(8,128)(2,1)}, bf16[400,512]{1,0:T(8,128)(2,1)S(1)}, u32[]{:S(2)}, u32[]{:S(2)}) collective-permute-start(bf16[400,512]{1,0:T(8,128)(2,1)} %param.18), channel_id=1, source_target_pairs={{0,4},{1,5},{2,6},{3,7},{4,0},{5,1},{6,2},{7,3},{8,12},{9,13},{10,... | collective-permute-start | bytes 1228808 | tf_op jit(solution)/shard_map/cond/branch_2_fun/ppermute | solution.py:143
  56.3 3.4 %copy-start.1 = (bf16[16,64,400]{2,1,0:T(8,128)(2,1)}, bf16[16,64,400]{2,1,0:T(8,128)(2,1)S(1)}, u32[]{:S(2)}) copy-start(bf16[16,64,400]{2,1,0:T(8,128)(2,1)S(1)} %all-to-all-done.1) | copy-start | bytes 2457604
  56.3 3.4 %collective-permute-start.45 = (bf16[16,64,400]{2,1,0:T(8,128)(2,1)S(1)}, bf16[16,64,400]{2,1,0:T(8,128)(2,1)S(1)}, u32[]{:S(2)}, u32[]{:S(2)}) collective-permute-start(bf16[16,64,400]{2,1,0:T(8,128)(2,1)S(1)} %all-to-all-done.1), channel_id=1, source_target_pairs={{0,1},{1,0},{2,3},{3,2},{4,5},{5,4},{6,7},{7,6},{8,9},{9,8},{10,11... | collective-permute-start | bytes 2457608 | tf_op jit(solution)/shard_map/ppermute | solution.py:143
  57.6 2.1 %collective-permute-start.44 = (bf16[400,512]{1,0:T(8,128)(2,1)}, bf16[400,512]{1,0:T(8,128)(2,1)S(1)}, u32[]{:S(2)}, u32[]{:S(2)}) collective-permute-start(bf16[400,512]{1,0:T(8,128)(2,1)} %get-tuple-element.137.pa_ref), channel_id=1, source_target_pairs={{0,1},{1,0},{2,3},{3,2},{4,5},{5,4},{6,7},{7,6},{8,9},{9,8},{10,11... | collective-permute-start | bytes 1228808 | tf_op jit(solution)/shard_map/ppermute | solution.py:143
  59.7 0.8 copy-start.5
  59.7 1.1 copy-start.3
  93.6 2.9 %collective-permute-start.46 = (bf16[16,64,400]{2,1,0:T(8,128)(2,1)}, bf16[16,64,400]{2,1,0:T(8,128)(2,1)S(1)}, u32[]{:S(2)}, u32[]{:S(2)}) collective-permute-start(bf16[16,64,400]{2,1,0:T(8,128)(2,1)} %bitcast.31), channel_id=1, source_target_pairs={{0,1},{1,0},{2,3},{3,2},{4,5},{5,4},{6,7},{7,6},{8,9},{9,8},{10,11... | collective-permute-start | bytes 2457608 | tf_op jit(solution)/shard_map/ppermute | solution.py:143
  96.5 9.8 %copy-start.4 = (bf16[400,512]{1,0:T(8,128)(2,1)S(1)}, bf16[400,512]{1,0:T(8,128)(2,1)}, u32[]{:S(2)}) copy-start(bf16[400,512]{1,0:T(8,128)(2,1)} %get-tuple-element.127) | copy-start | bytes 1228804
  99.1 34.2 %all-to-all-start.2 = ((bf16[16,64,400]{2,1,0:T(8,128)(2,1)}), bf16[16,64,400]{2,1,0:T(8,128)(2,1)S(1)}, u32[]{:S(2)}, u32[]{:S(2)}) async-start(bf16[16,64,400]{2,1,0:T(8,128)(2,1)} %fusion), calls=%async_computation.2 | async-start | bytes 2097152 | tf_op jit(solution)/shard_map/all_to_all | solution.py:153
  106.3 5.0 %collective-permute-start.47 = (bf16[400,512]{1,0:T(8,128)(2,1)S(1)}, bf16[400,512]{1,0:T(8,128)(2,1)S(1)}, u32[]{:S(2)}, u32[]{:S(2)}) collective-permute-start(bf16[400,512]{1,0:T(8,128)(2,1)S(1)} %copy-done.4), channel_id=1, source_target_pairs={{0,1},{1,0},{2,3},{3,2},{4,5},{5,4},{6,7},{7,6},{8,9},{9,8},{10,11... | collective-permute-start | bytes 1228808 | tf_op jit(solution)/shard_map/ppermute | solution.py:143
  111.4 21.6 %collective-permute-start.23 = (bf16[400,512]{1,0:T(8,128)(2,1)S(1)}, bf16[400,512]{1,0:T(8,128)(2,1)S(1)}, u32[]{:S(2)}, u32[]{:S(2)}) collective-permute-start(bf16[400,512]{1,0:T(8,128)(2,1)S(1)} %param.26), channel_id=1, source_target_pairs={{0,4},{1,5},{2,6},{3,7},{4,0},{5,1},{6,2},{7,3},{8,12},{9,13},{10,... | collective-permute-start | bytes 1228808 | tf_op jit(solution)/shard_map/cond/branch_2_fun/ppermute | solution.py:143
  134.1 21.7 %all-to-all-start.3 = ((bf16[8,8,400]{2,1,0:T(8,128)(2,1)}), bf16[8,8,400]{2,1,0:T(8,128)(2,1)S(1)}, u32[]{:S(2)}, u32[]{:S(2)}) async-start(bf16[8,8,400]{2,1,0:T(8,128)(2,1)} %bitcast.16), calls=%async_computation.3 | async-start | bytes 131072 | tf_op jit(solution)/shard_map/all_to_all | solution.py:153
  138.6 15.3 %copy-start = (f32[400,512]{1,0:T(8,128)S(1)}, f32[400,512]{1,0:T(8,128)}, u32[]{:S(2)}) copy-start(f32[400,512]{1,0:T(8,128)} %last.1) | copy-start | bytes 2457604
  138.6 15.5 %copy-start.9 = (f32[512]{0:T(512)S(1)}, f32[512]{0:T(512)}, u32[]{:S(2)}) copy-start(f32[512]{0:T(512)} %param.59) | copy-start | bytes 6148
  138.6 16.0 %copy-start.2 = (f32[512,400]{0,1:T(8,128)S(1)}, f32[512,400]{0,1:T(8,128)}, u32[]{:S(2)}) copy-start(f32[512,400]{0,1:T(8,128)} %param.58) | copy-start | bytes 2457604
  138.7 15.2 %collective-permute-start.38 = (bf16[400,512]{1,0:T(8,128)(2,1)S(1)}, bf16[400,512]{1,0:T(8,128)(2,1)S(1)}, u32[]{:S(2)}, u32[]{:S(2)}) collective-permute-start(bf16[400,512]{1,0:T(8,128)(2,1)S(1)} %param.42), channel_id=1, source_target_pairs={{0,160},{1,161},{2,162},{3,163},{4,164},{5,165},{6,166},{7,167},{8... | collective-permute-start | bytes 1228808 | tf_op jit(solution)/shard_map/cond/branch_10_fun/ppermute | solution.py:143
  153.9 2.0 %copy-start.10 = (f32[8]{0:T(128)S(1)}, f32[8]{0:T(128)}, u32[]{:S(2)}) copy-start(f32[8]{0:T(128)} %param.61) | copy-start | bytes 100
  153.9 2.5 %copy-start.6 = (f32[8,400]{1,0:T(8,128)S(1)}, f32[8,400]{1,0:T(8,128)}, u32[]{:S(2)}) copy-start(f32[8,400]{1,0:T(8,128)} %param.60) | copy-start | bytes 38404

commit v2 on v1

--- a/solution.py
+++ b/solution.py
@@ -15,6 +15,7 @@
 
 
 TILE = 256
+VL = 50
 
 
 def dot(a, b, dims):
@@ -36,34 +37,61 @@
     return (lax.broadcasted_iota(jnp.int32, (n, n), 0) == lax.broadcasted_iota(jnp.int32, (n, n), 1)).astype(BF)
 
 
-def train_kernel(odd_ref, bt_ref, pa_ref, pb_ref, r0_ref, r1_ref, s_ref, r_ref, d_ref, n_ref, rall_ref,
+def line(values):
+    return jnp.concatenate([values[i:i + 1] for i in range(values.shape[0])], axis=1)
+
+
+def live_sources(count_ref, s_ref):
+    lines, lanes = s_ref.shape
+    edge = lax.broadcasted_iota(jnp.int32, (lines, lanes), 0) * lanes + lax.broadcasted_iota(jnp.int32, (lines, lanes), 1)
+    return jnp.where(edge < count_ref[0], s_ref[...], -1)
+
+
+def train_kernel(odd_ref, core_ref, count_ref, bt_in, pa_in, pb_in, r0_in, r1_in, sid_in, rid_in, d_in, n_in,
                  part_ref, xo_ref, g0_ref, g1_ref,
-                 rt, pt, p, own, rl, qa, wa, xr, times_all, sc0, sc1):
+                 rt, pt, p, own, rl, qa, wa, xr, times_all, sc0, sc1, s_ref, r_ref, rall,
+                 bt_ref, pa_ref, pb_ref, table, sid_ref, rid_ref, d_ref, n_ref, sems):
+    half = r0_in.shape[0]
+    moves = [
+        pltpu.make_async_copy(source, target, sems.at[i])
+        for i, (source, target) in enumerate((
+            (pa_in, pa_ref), (pb_in, pb_ref), (sid_in, sid_ref), (rid_in, rid_ref),
+            (r0_in, table.at[pl.ds(0, half)]), (r1_in, table.at[pl.ds(half, half)]),
+            (bt_in, bt_ref), (n_in, n_ref), (d_in, d_ref)))
+    ]
+    for move in moves:
+        move.start()
     width, rows = pa_ref.shape
     groups, negs = n_ref.shape
-    edges = rall_ref.shape[1]
+    edges = rall.shape[1]
     glen = edges // groups
-    half = r0_ref.shape[0]
     rels = 2 * half
+    for move in moves[:4]:
+        move.wait()
+    s_ref[...] = live_sources(count_ref, sid_ref)
+    rid = rid_ref[...]
+    core = jnp.bitwise_and(jnp.bitwise_xor(jnp.right_shift(rid, 3), core_ref[0]), 1)
+    spot = core * half + jnp.right_shift(rid, 4) * 8 + jnp.bitwise_and(rid, 7)
+    r_ref[...] = spot
+    rall[...] = line(spot)
     ident = identity(width)
-    wide = TILE
     pt[...] = jnp.where(odd_ref[0] == 1, pb_ref[...], pa_ref[...])
     p[...] = (0.5 * pt[...].astype(F32)).T.astype(BF)
-    for k, ref in enumerate((r0_ref, r1_ref)):
-        def turn(t, carry, k=k, ref=ref):
-            at = pl.multiple_of(t * wide, wide)
-            rt[:, pl.ds(k * half + at, wide)] = dot(ident, ref[pl.ds(at, wide), :], NT).astype(BF)
-            return carry
-
-        lax.fori_loop(0, half // wide, turn, 0)
+    for move in moves[4:]:
+        move.wait()
+
+    def turn(t, carry):
+        at = pl.ds(pl.multiple_of(t * TILE, TILE), TILE)
+        rt[:, at] = dot(ident, table[at, :], NT).astype(BF)
+        return carry
+
+    lax.fori_loop(0, rels // TILE, turn, 0)
 
     def span(g):
         return pl.ds(pl.multiple_of(g * glen, glen), glen)
 
     def ids(ref, g):
-        lines = glen // 128
-        got = ref[pl.ds(g * lines, lines), :]
-        return jnp.concatenate([got[i:i + 1] for i in range(lines)], axis=1)
+        return line(ref[pl.ds(g * (glen // 128), glen // 128), :])
 
     def forward(g, sc):
         mine = dot(bt_ref[...], one_hots(ids(s_ref, g), rows), NN).astype(BF)
@@ -114,7 +142,7 @@
     tiles = half // TILE
 
     def scatter(t, carry):
-        out = dot(xr[...], one_hot(rall_ref[...], t), NT).T.astype(BF)
+        out = dot(xr[...], one_hot(rall[...], t), NT).T.astype(BF)
         at = pl.ds(pl.multiple_of(lax.rem(t, tiles) * TILE, TILE), TILE)
 
         @pl.when(t < tiles)
@@ -130,9 +158,11 @@
     lax.fori_loop(0, rels // TILE, scatter, 0)
 
 
-def last_kernel(xo_ref, sall_ref, own_ref):
+def last_kernel(count_ref, xo_ref, sid_ref, own_ref):
+    sall = line(live_sources(count_ref, sid_ref))
+
     def onto_rows(t, carry):
-        own_ref[:, pl.ds(pl.multiple_of(t * TILE, TILE), TILE)] = dot(xo_ref[...], one_hot(sall_ref[...], t), NT)
+        own_ref[:, pl.ds(pl.multiple_of(t * TILE, TILE), TILE)] = dot(xo_ref[...], one_hot(sall, t), NT)
         return carry
 
     lax.fori_loop(0, own_ref.shape[1] // TILE, onto_rows, 0)
@@ -187,6 +217,7 @@
     z_size, xy_size = 1 << Z_BITS, 1 << XY_BITS
     half = z_size * xy_size * rel_local
     vm = pl.BlockSpec(memory_space=pltpu.VMEM)
+    sm = pl.BlockSpec(memory_space=pltpu.SMEM)
     sh = jax.ShapeDtypeStruct
 
     own_t = embeddings.astype(BF).T
@@ -204,32 +235,32 @@
     rel_there = swap(rel_here, 1)
     part_there = swap(part_t, 1)
 
-    owner = relation_ids // rel_local
-    core = jnp.bitwise_and(jnp.bitwise_xor(owner, me), 1)
-    spot = core * half + jnp.right_shift(owner, CORE_BITS) * rel_local + relation_ids % rel_local
-
-    live_sources = jnp.where(jnp.arange(edges, dtype=jnp.int32) < edge_count[0], source_rows, -1)
-
+    lines = (edges // 128, 128)
     part_grad, to_source, grad_here, grad_there = pl.pallas_call(
         train_kernel,
         out_shape=(sh((width, rows), BF), sh((width, edges), BF), sh((half, width), BF), sh((half, width), BF)),
-        in_specs=[pl.BlockSpec(memory_space=pltpu.SMEM)] + [vm] * 10, out_specs=(vm,) * 4,
+        in_specs=[sm] * 3 + [pl.BlockSpec(memory_space=pltpu.HBM)] * 9, out_specs=(vm,) * 4,
         scratch_shapes=[pltpu.VMEM((width, 2 * half), BF), pltpu.VMEM((width, rows), BF), pltpu.VMEM((rows, width), BF),
                         *[pltpu.VMEM((width, edges), BF)] * 3, pltpu.VMEM((rows, edges), BF), pltpu.VMEM((width, edges), BF),
-                        pltpu.VMEM((groups, rows, 128), BF),
-                        pltpu.VMEM((rows, edges // groups), F32), pltpu.VMEM((rows, edges // groups), F32)],
+                        pltpu.VMEM((groups, rows, 128), BF), pltpu.VMEM((rows, edges // groups), F32),
+                        pltpu.VMEM((rows, edges // groups), F32), pltpu.VMEM(lines, jnp.int32),
+                        pltpu.VMEM(lines, jnp.int32), pltpu.VMEM((1, edges), jnp.int32),
+                        *[pltpu.VMEM((width, rows), BF)] * 3, pltpu.VMEM((2 * half, width), BF),
+                        *[pltpu.VMEM(lines, jnp.int32)] * 3, pltpu.VMEM(negative_rows.shape, jnp.int32),
+                        pltpu.SemaphoreType.DMA((9,))],
+        compiler_params=pltpu.CompilerParams(vmem_limit_bytes=VL << 20),
         name="train",
-    )(jnp.bitwise_and(partner_mask, 1), own_t, part_t, part_there,
+    )(jnp.bitwise_and(partner_mask, 1), jnp.bitwise_and(me, 1).reshape(1), edge_count, own_t, part_t, part_there,
       rel_here.reshape(half, width), rel_there.reshape(half, width),
-      live_sources.reshape(-1, 128), spot.reshape(-1, 128), dest_rows.reshape(-1, 128), negative_rows,
-      spot.reshape(1, edges))
+      source_rows.reshape(lines), relation_ids.reshape(lines), dest_rows.reshape(lines), negative_rows)
 
     by_z = (xy_size, z_size * rel_local, width)
     from_core = swap(grad_there.reshape(by_z), 1)
     part_core = swap(part_grad, 1)
     own_grad = pl.pallas_call(
-        last_kernel, out_shape=sh((width, rows), F32), in_specs=[vm] * 2, out_specs=vm, name="last",
-    )(to_source, live_sources.reshape(1, edges))
+        last_kernel, out_shape=sh((width, rows), F32), in_specs=[sm] + [vm] * 2, out_specs=vm, name="last",
+        compiler_params=pltpu.CompilerParams(vmem_limit_bytes=16 << 20),
+    )(edge_count, to_source, source_rows.reshape(lines))
     returned = jnp.where(odd, part_core, part_grad)
     grad_sum = (grad_here.reshape(by_z).astype(F32) + from_core.astype(F32)).astype(BF)
     grad_xy = added(exchange(grad_sum, XY_SHIFT, XY_BITS))

time: 158 us -> 154 us (0.975)
  Pallas kernels: 37 us -> 33.4 us
  waiting for transfers between devices: 61.9 us -> 63.7 us
    pallas_call x1, Pallas kernels: 4.26 us -> 1.69 us  [local(): pl.pallas_call(last_kernel, out_shape=sh((width, rows), F32), in_specs=[s...]
    ppermute x8, waiting for transfers between devices: 61.9 us -> 63.7 us  [swap(): return lax.ppermute(value, 'dom', pairs)]
  transfers between devices with their start and end apart: 12 -> 12, of which waited for: 6 -> 7; matrix products, arithmetic and copies ran while one was open for 4% -> 3% of each run, Pallas kernels for 3% -> 1%
where the time goes in v2:
time: 154 us; the launch traced here: 153 us
  waiting for transfers between devices  63.7 us (41%)
  starting transfers between devices  40.7 us (26%)
  Pallas kernels  33.4 us (22%)
  other arithmetic  9.47 us (6%)
  local copies, waits for them, and re-layouts  3.62 us (2%)
  between operations  2.08 us (1%)
    ppermute x8, waiting for transfers between devices, swap(): return lax.ppermute(value, 'dom', pairs)  63.7 us
    pallas_call x1, Pallas kernels, local(): pl.pallas_call(train_kernel, out_shape=(sh((width, rows), BF), sh((width,...  31.7 us
    all_to_all x4, starting transfers between devices, exchange(): lax.all_to_all(blocks, 'dom', 0, 0, axis_index_groups=groups_of(shift, bi...  27.8 us
    ppermute x8, starting transfers between devices, swap(): return lax.ppermute(value, 'dom', pairs)  13 us
  transfers between devices with their start and end apart: 12, of which 7 were waited for; matrix products, arithmetic and copies ran while one was open for 3% of the time, Pallas kernels for 1%

profile of v2, /device:TPU:2, one launch (start us, length us, event | category | flops | bytes accessed | tf_op | source)
XLA Modules:
  0.0 153.3 jit_solution(15215632992111166098)
XLA Ops:
  0.6 0.7 convert_element_type.61
  1.4 0.6 broadcast_in_dim.4
  2.0 8.5 %all-to-all-start = ((bf16[8,8,400]{2,1,0:T(8,128)(2,1)}), bf16[8,8,400]{2,1,0:T(8,128)(2,1)S(1)}, u32[]{:S(2)}, u32[]{:S(2)}) async-start(bf16[8,8,400]{2,1,0:T(8,128)(2,1)} %broadcast_in_dim.4), calls=%async_computation | async-start | bytes 131072 | tf_op jit(solution)/shard_map/all_to_all | solution.py:183
  10.5 1.2 convert_bitcast_fusion.bt_in
  12.3 15.1 %conditional.4 = (bf16[400,512]{1,0:T(8,128)(2,1)}) conditional(s32[]{:T(128)} %bitcast.3, bf16[400,512]{1,0:T(8,128)(2,1)S(1)} %convert_bitcast_fusion.bt_in, bf16[400,512]{1,0:T(8,128)(2,1)S(1)} %convert_bitcast_fusion.bt_in, bf16[400,512]{1,0:T(8,128)(2,1)S(1)} %convert_bitcast_fusion.bt_in, ...), branch_computations={%region_0.0_spmd, %region_1.0_spmd, %region_2.0_spmd, %region_3.0_... | conditional | bytes 1638448 | solution.py:191
  12.3 4.8 %collective-permute-start.9 = (bf16[400,512]{1,0:T(8,128)(2,1)S(1)}, bf16[400,512]{1,0:T(8,128)(2,1)}, u32[]{:S(2)}, u32[]{:S(2)}) collective-permute-start(bf16[400,512]{1,0:T(8,128)(2,1)S(1)} %param.10), channel_id=1, source_target_pairs={{0,160},{1,161},{2,162},{3,163},{4,164},{5,165},{6,166},{7,167},{8... | collective-permute-start | bytes 1228808 | tf_op jit(solution)/shard_map/cond/branch_10_fun/ppermute | solution.py:173
  17.2 10.2 %collective-permute-done.9 = bf16[400,512]{1,0:T(8,128)(2,1)} collective-permute-done((bf16[400,512]{1,0:T(8,128)(2,1)S(1)}, bf16[400,512]{1,0:T(8,128)(2,1)}, u32[]{:S(2)}, u32[]{:S(2)}) %collective-permute-start.9) | collective-permute-done | bytes 409632 | tf_op jit(solution)/shard_map/cond/branch_10_fun/ppermute | solution.py:173
  27.4 1.1 broadcast_in_dim.5
  28.5 7.5 %all-to-all-start.1 = ((bf16[16,64,400]{2,1,0:T(8,128)(2,1)}), bf16[16,64,400]{2,1,0:T(8,128)(2,1)S(1)}, u32[]{:S(2)}, u32[]{:S(2)}) async-start(bf16[16,64,400]{2,1,0:T(8,128)(2,1)} %broadcast_in_dim.5), calls=%async_computation.1 | async-start | bytes 2097152 | tf_op jit(solution)/shard_map/all_to_all | solution.py:183
  36.0 20.3 %conditional.5 = (bf16[400,512]{1,0:T(8,128)(2,1)}) conditional(s32[]{:T(128)} %bitcast.4, bf16[400,512]{1,0:T(8,128)(2,1)} %get-tuple-element.136, bf16[400,512]{1,0:T(8,128)(2,1)} %get-tuple-element.136, bf16[400,512]{1,0:T(8,128)(2,1)} %get-tuple-element.136, bf16[400,512]{1,0:T(8,128)(2,1)} %get-tuple-element.136, ...), branch_computations={%region_16.0_spmd, %region_17.0_spmd, %region_18.0_spmd, %region_1... | conditional | bytes 2457648 | solution.py:191
  36.1 2.7 %collective-permute-start.16 = (bf16[400,512]{1,0:T(8,128)(2,1)}, bf16[400,512]{1,0:T(8,128)(2,1)S(1)}, u32[]{:S(2)}, u32[]{:S(2)}) collective-permute-start(bf16[400,512]{1,0:T(8,128)(2,1)} %param.18), channel_id=1, source_target_pairs={{0,4},{1,5},{2,6},{3,7},{4,0},{5,1},{6,2},{7,3},{8,12},{9,13},{10,... | collective-permute-start | bytes 1228808 | tf_op jit(solution)/shard_map/cond/branch_2_fun/ppermute | solution.py:173
  38.8 16.8 %collective-permute-done.16 = bf16[400,512]{1,0:T(8,128)(2,1)S(1)} collective-permute-done((bf16[400,512]{1,0:T(8,128)(2,1)}, bf16[400,512]{1,0:T(8,128)(2,1)S(1)}, u32[]{:S(2)}, u32[]{:S(2)}) %collective-permute-start.16) | collective-permute-done | bytes 409632 | tf_op jit(solution)/shard_map/cond/branch_2_fun/ppermute | solution.py:173
  55.5 0.8 copy.32
  57.5 2.1 %collective-permute-done.44.pb_in = bf16[400,512]{1,0:T(8,128)(2,1)S(1)} collective-permute-done((bf16[400,512]{1,0:T(8,128)(2,1)}, bf16[400,512]{1,0:T(8,128)(2,1)S(1)}, u32[]{:S(2)}, u32[]{:S(2)}) %collective-permute-start.44) | collective-permute-done | bytes 409632 | tf_op jit(solution)/shard_map/ppermute | solution.py:173
  59.6 1.0 copy-done.6
  60.6 31.7 %train.1 = (bf16[400,512]{1,0:T(8,128)(2,1)}, bf16[400,3072]{1,0:T(8,128)(2,1)}, bf16[1024,400]{1,0:T(8,128)(2,1)S(1)}, bf16[1024,400]{1,0:T(8,128)(2,1)S(1)}) custom-call(s32[1]{0:T(128)S(6)} %and.19.odd_ref, s32[1]{0:T(128)} %bitcast.core_ref, s32[1]{0:T(128)S(6)} %copy.63.count_ref, bf16[400,512]{1,0:T(8,128)(2,1)S(1)} %convert_bitcast_fusion.bt_in, ...), custom_call_target="tpu_custom_call" | custom-call | tf_op jit(solution)/shard_map/train/pallas_call | solution.py:239
  92.5 2.5 %collective-permute-done.46 = bf16[16,64,400]{2,1,0:T(8,128)(2,1)S(1)} collective-permute-done((bf16[16,64,400]{2,1,0:T(8,128)(2,1)S(1)}, bf16[16,64,400]{2,1,0:T(8,128)(2,1)S(1)}, u32[]{:S(2)}, u32[]{:S(2)}) %collective-permute-start.46) | collective-permute-done | bytes 819232 | tf_op jit(solution)/shard_map/ppermute | solution.py:173
  95.0 1.3 fusion
  96.3 7.2 %all-to-all-start.2 = ((bf16[16,64,400]{2,1,0:T(8,128)(2,1)}), bf16[16,64,400]{2,1,0:T(8,128)(2,1)}, u32[]{:S(2)}, u32[]{:S(2)}) async-start(bf16[16,64,400]{2,1,0:T(8,128)(2,1)} %fusion), calls=%async_computation.2 | async-start | bytes 2097152 | tf_op jit(solution)/shard_map/all_to_all | solution.py:183
  103.5 1.7 %last.1 = f32[400,512]{1,0:T(8,128)S(1)} custom-call(s32[1]{0:T(128)S(6)} %copy.63.count_ref, bf16[400,3072]{1,0:T(8,128)(2,1)S(1)} %copy-done, s32[24,128]{1,0:T(8,128)S(1)} %bitcast.21), custom_call_target="tpu_custom_call" | custom-call | tf_op jit(solution)/shard_map/last/pallas_call | solution.py:260
  105.5 1.0 broadcast_select_fusion
  106.5 21.7 %conditional.6 = (bf16[400,512]{1,0:T(8,128)(2,1)S(1)}) conditional(s32[]{:T(128)} %bitcast.4, bf16[400,512]{1,0:T(8,128)(2,1)S(1)} %broadcast_select_fusion, bf16[400,512]{1,0:T(8,128)(2,1)S(1)} %broadcast_select_fusion, bf16[400,512]{1,0:T(8,128)(2,1)S(1)} %broadcast_select_fusion, ...), branch_computations={%region_25.26_spmd, %region_26.27_spmd, %region_27.28_spmd, %regio... | conditional | bytes 2457648 | solution.py:191
  106.7 21.3 %collective-permute-done.23 = bf16[400,512]{1,0:T(8,128)(2,1)S(1)} collective-permute-done((bf16[400,512]{1,0:T(8,128)(2,1)S(1)}, bf16[400,512]{1,0:T(8,128)(2,1)S(1)}, u32[]{:S(2)}, u32[]{:S(2)}) %collective-permute-start.23) | collective-permute-done | bytes 409632 | tf_op jit(solution)/shard_map/cond/branch_2_fun/ppermute | solution.py:173
  128.2 2.0 %reduce_sum.39 = bf16[64,400]{1,0:T(8,128)(2,1)} reduce(bf16[16,64,400]{2,1,0:T(8,128)(2,1)} %all-to-all-done.2, bf16[]{:T(256)} %constant.34.clone.1), dimensions={0}, to_apply=%region_24.25 | reduce | flops 384000 | bytes 870402 | tf_op jit(solution)/shard_map/reduce_sum | solution.py:195
  130.3 4.6 %all-to-all-start.3 = ((bf16[8,8,400]{2,1,0:T(8,128)(2,1)}), bf16[8,8,400]{2,1,0:T(8,128)(2,1)S(1)}, u32[]{:S(2)}, u32[]{:S(2)}) async-start(bf16[8,8,400]{2,1,0:T(8,128)(2,1)} %bitcast.14), calls=%async_computation.3 | async-start | bytes 131072 | tf_op jit(solution)/shard_map/all_to_all | solution.py:183
  134.9 15.2 %conditional.7 = (bf16[400,512]{1,0:T(8,128)(2,1)S(1)}) conditional(s32[]{:T(128)} %bitcast.3, bf16[400,512]{1,0:T(8,128)(2,1)S(1)} %get-tuple-element.138, bf16[400,512]{1,0:T(8,128)(2,1)S(1)} %get-tuple-element.138, bf16[400,512]{1,0:T(8,128)(2,1)S(1)} %get-tuple-element.138, ...), branch_computations={%region_33.34_spmd, %region_34.35_spmd, %region_35.36_spmd, %regio... | conditional | bytes 2457648 | solution.py:191
  134.9 4.6 %collective-permute-start.38 = (bf16[400,512]{1,0:T(8,128)(2,1)S(1)}, bf16[400,512]{1,0:T(8,128)(2,1)S(1)}, u32[]{:S(2)}, u32[]{:S(2)}) collective-permute-start(bf16[400,512]{1,0:T(8,128)(2,1)S(1)} %param.42), channel_id=1, source_target_pairs={{0,160},{1,161},{2,162},{3,163},{4,164},{5,165},{6,166},{7,167},{8... | collective-permute-start | bytes 1228808 | tf_op jit(solution)/shard_map/cond/branch_10_fun/ppermute | solution.py:173
  139.5 10.6 %collective-permute-done.38 = bf16[400,512]{1,0:T(8,128)(2,1)S(1)} collective-permute-done((bf16[400,512]{1,0:T(8,128)(2,1)S(1)}, bf16[400,512]{1,0:T(8,128)(2,1)S(1)}, u32[]{:S(2)}, u32[]{:S(2)}) %collective-permute-start.38) | collective-permute-done | bytes 409632 | tf_op jit(solution)/shard_map/cond/branch_10_fun/ppermute | solution.py:173
  150.3 0.6 fusion.2
  150.9 1.1 bitcast_subtract_fusion
  152.1 0.5 fusion.1
  152.6 0.7 divide_subtract_fusion
  (35 shorter events, 1.5 us)
Async XLA Ops:
  2.0 25.4 %all-to-all-start = ((bf16[8,8,400]{2,1,0:T(8,128)(2,1)}), bf16[8,8,400]{2,1,0:T(8,128)(2,1)S(1)}, u32[]{:S(2)}, u32[]{:S(2)}) async-start(bf16[8,8,400]{2,1,0:T(8,128)(2,1)} %broadcast_in_dim.4), calls=%async_computation | async-start | bytes 131072 | tf_op jit(solution)/shard_map/all_to_all | solution.py:183
  12.3 15.0 %collective-permute-start.9 = (bf16[400,512]{1,0:T(8,128)(2,1)S(1)}, bf16[400,512]{1,0:T(8,128)(2,1)}, u32[]{:S(2)}, u32[]{:S(2)}) collective-permute-start(bf16[400,512]{1,0:T(8,128)(2,1)S(1)} %param.10), channel_id=1, source_target_pairs={{0,160},{1,161},{2,162},{3,163},{4,164},{5,165},{6,166},{7,167},{8... | collective-permute-start | bytes 1228808 | tf_op jit(solution)/shard_map/cond/branch_10_fun/ppermute | solution.py:173
  28.5 27.8 %all-to-all-start.1 = ((bf16[16,64,400]{2,1,0:T(8,128)(2,1)}), bf16[16,64,400]{2,1,0:T(8,128)(2,1)S(1)}, u32[]{:S(2)}, u32[]{:S(2)}) async-start(bf16[16,64,400]{2,1,0:T(8,128)(2,1)} %broadcast_in_dim.5), calls=%async_computation.1 | async-start | bytes 2097152 | tf_op jit(solution)/shard_map/all_to_all | solution.py:183
  36.0 24.6 %copy-start.1 = (s32[3072]{0:T(1024)S(1)}, s32[3072]{0:T(1024)}, u32[]{:S(2)}) copy-start(s32[3072]{0:T(1024)} %param.63) | copy-start | bytes 36868
  36.0 24.6 %copy-start.2 = (s32[12,512]{1,0:T(8,128)S(1)}, s32[12,512]{1,0:T(8,128)}, u32[]{:S(2)}) copy-start(s32[12,512]{1,0:T(8,128)} %n_in.1) | copy-start | bytes 73732
  36.0 24.6 %copy-start.3 = (s32[3072]{0:T(1024)S(1)}, s32[3072]{0:T(1024)}, u32[]{:S(2)}) copy-start(s32[3072]{0:T(1024)} %param.64) | copy-start | bytes 36868
  36.0 24.5 %copy-start.4 = (s32[3072]{0:T(1024)S(1)}, s32[3072]{0:T(1024)}, u32[]{:S(2)}) copy-start(s32[3072]{0:T(1024)} %param.65) | copy-start | bytes 36868
  36.1 19.5 %collective-permute-start.16 = (bf16[400,512]{1,0:T(8,128)(2,1)}, bf16[400,512]{1,0:T(8,128)(2,1)S(1)}, u32[]{:S(2)}, u32[]{:S(2)}) collective-permute-start(bf16[400,512]{1,0:T(8,128)(2,1)} %param.18), channel_id=1, source_target_pairs={{0,4},{1,5},{2,6},{3,7},{4,0},{5,1},{6,2},{7,3},{8,12},{9,13},{10,... | collective-permute-start | bytes 1228808 | tf_op jit(solution)/shard_map/cond/branch_2_fun/ppermute | solution.py:173
  56.3 3.2 %collective-permute-start.45 = (bf16[16,64,400]{2,1,0:T(8,128)(2,1)S(1)}, bf16[16,64,400]{2,1,0:T(8,128)(2,1)S(1)}, u32[]{:S(2)}, u32[]{:S(2)}) collective-permute-start(bf16[16,64,400]{2,1,0:T(8,128)(2,1)S(1)} %all-to-all-done.1), channel_id=1, source_target_pairs={{0,1},{1,0},{2,3},{3,2},{4,5},{5,4},{6,7},{7,6},{8,9},{9,8},{10,11... | collective-permute-start | bytes 2457608 | tf_op jit(solution)/shard_map/ppermute | solution.py:173
  56.3 3.2 %collective-permute-start.44 = (bf16[400,512]{1,0:T(8,128)(2,1)}, bf16[400,512]{1,0:T(8,128)(2,1)S(1)}, u32[]{:S(2)}, u32[]{:S(2)}) collective-permute-start(bf16[400,512]{1,0:T(8,128)(2,1)} %get-tuple-element.137.pa_in), channel_id=1, source_target_pairs={{0,1},{1,0},{2,3},{3,2},{4,5},{5,4},{6,7},{7,6},{8,9},{9,8},{10,11... | collective-permute-start | bytes 1228808 | tf_op jit(solution)/shard_map/ppermute | solution.py:173
  59.6 1.0 copy-start.6
  92.2 2.7 %collective-permute-start.46 = (bf16[16,64,400]{2,1,0:T(8,128)(2,1)S(1)}, bf16[16,64,400]{2,1,0:T(8,128)(2,1)S(1)}, u32[]{:S(2)}, u32[]{:S(2)}) collective-permute-start(bf16[16,64,400]{2,1,0:T(8,128)(2,1)S(1)} %bitcast.24), channel_id=1, source_target_pairs={{0,1},{1,0},{2,3},{3,2},{4,5},{5,4},{6,7},{7,6},{8,9},{9,8},{10,11... | collective-permute-start | bytes 2457608 | tf_op jit(solution)/shard_map/ppermute | solution.py:173
  95.0 8.5 %copy-start = (bf16[400,3072]{1,0:T(8,128)(2,1)S(1)}, bf16[400,3072]{1,0:T(8,128)(2,1)}, u32[]{:S(2)}) copy-start(bf16[400,3072]{1,0:T(8,128)(2,1)} %get-tuple-element.128.xo_ref) | copy-start | bytes 7372804
  96.3 31.9 %all-to-all-start.2 = ((bf16[16,64,400]{2,1,0:T(8,128)(2,1)}), bf16[16,64,400]{2,1,0:T(8,128)(2,1)}, u32[]{:S(2)}, u32[]{:S(2)}) async-start(bf16[16,64,400]{2,1,0:T(8,128)(2,1)} %fusion), calls=%async_computation.2 | async-start | bytes 2097152 | tf_op jit(solution)/shard_map/all_to_all | solution.py:183
  103.5 2.0 %collective-permute-start.47 = (bf16[400,512]{1,0:T(8,128)(2,1)}, bf16[400,512]{1,0:T(8,128)(2,1)S(1)}, u32[]{:S(2)}, u32[]{:S(2)}) collective-permute-start(bf16[400,512]{1,0:T(8,128)(2,1)} %get-tuple-element.127), channel_id=1, source_target_pairs={{0,1},{1,0},{2,3},{3,2},{4,5},{5,4},{6,7},{7,6},{8,9},{9,8},{10,11... | collective-permute-start | bytes 1228808 | tf_op jit(solution)/shard_map/ppermute | solution.py:173
  106.6 21.4 %collective-permute-start.23 = (bf16[400,512]{1,0:T(8,128)(2,1)S(1)}, bf16[400,512]{1,0:T(8,128)(2,1)S(1)}, u32[]{:S(2)}, u32[]{:S(2)}) collective-permute-start(bf16[400,512]{1,0:T(8,128)(2,1)S(1)} %param.26), channel_id=1, source_target_pairs={{0,4},{1,5},{2,6},{3,7},{4,0},{5,1},{6,2},{7,3},{8,12},{9,13},{10,... | collective-permute-start | bytes 1228808 | tf_op jit(solution)/shard_map/cond/branch_2_fun/ppermute | solution.py:173
  130.3 21.7 %all-to-all-start.3 = ((bf16[8,8,400]{2,1,0:T(8,128)(2,1)}), bf16[8,8,400]{2,1,0:T(8,128)(2,1)S(1)}, u32[]{:S(2)}, u32[]{:S(2)}) async-start(bf16[8,8,400]{2,1,0:T(8,128)(2,1)} %bitcast.14), calls=%async_computation.3 | async-start | bytes 131072 | tf_op jit(solution)/shard_map/all_to_all | solution.py:183
  134.8 15.4 %copy-start.8 = (f32[512]{0:T(512)S(1)}, f32[512]{0:T(512)}, u32[]{:S(2)}) copy-start(f32[512]{0:T(512)} %param.59) | copy-start | bytes 6148
  134.8 16.0 %copy-start.5 = (f32[512,400]{0,1:T(8,128)S(1)}, f32[512,400]{0,1:T(8,128)}, u32[]{:S(2)}) copy-start(f32[512,400]{0,1:T(8,128)} %param.58) | copy-start | bytes 2457604
  134.9 15.1 %collective-permute-start.38 = (bf16[400,512]{1,0:T(8,128)(2,1)S(1)}, bf16[400,512]{1,0:T(8,128)(2,1)S(1)}, u32[]{:S(2)}, u32[]{:S(2)}) collective-permute-start(bf16[400,512]{1,0:T(8,128)(2,1)S(1)} %param.42), channel_id=1, source_target_pairs={{0,160},{1,161},{2,162},{3,163},{4,164},{5,165},{6,166},{7,167},{8... | collective-permute-start | bytes 1228808 | tf_op jit(solution)/shard_map/cond/branch_10_fun/ppermute | solution.py:173
  150.1 2.0 %copy-start.9 = (f32[8]{0:T(128)S(1)}, f32[8]{0:T(128)}, u32[]{:S(2)}) copy-start(f32[8]{0:T(128)} %param.61) | copy-start | bytes 100
  150.1 2.5 %copy-start.7 = (f32[8,400]{1,0:T(8,128)S(1)}, f32[8,400]{1,0:T(8,128)}, u32[]{:S(2)}) copy-start(f32[8,400]{1,0:T(8,128)} %param.60) | copy-start | bytes 38404

commit v3 on v2

--- a/solution.py
+++ b/solution.py
@@ -115,8 +115,9 @@
         pos_grad = 0.5 * jnp.tanh(positive) - 0.5
         times = times_all[pl.ds(g, 1)][0].astype(F32)
         times = jnp.concatenate([times, times], axis=1)
-        weight = (jnp.tanh(score) + 1.0) * times
-        weight = jnp.where(hit, weight + pos_grad, weight).astype(BF)
+        weight = (jnp.tanh(sc[...]) + 1.0) * times
+        again = (row + rows) == (ids(d_ref, g) + rows)
+        weight = (weight + jnp.where(again, pos_grad, 0.0)).astype(BF)
         wa[:, span(g)] = weight
         grad = dot(pt[...], weight, NN).astype(BF)
         xo_ref[:, span(g)] = grad * rl[:, span(g)]
@@ -248,7 +249,8 @@
                         *[pltpu.VMEM((width, rows), BF)] * 3, pltpu.VMEM((2 * half, width), BF),
                         *[pltpu.VMEM(lines, jnp.int32)] * 3, pltpu.VMEM(negative_rows.shape, jnp.int32),
                         pltpu.SemaphoreType.DMA((9,))],
-        compiler_params=pltpu.CompilerParams(vmem_limit_bytes=VL << 20),
+        compiler_params=pltpu.CompilerParams(
+            vmem_limit_bytes=VL << 20),
         name="train",
     )(jnp.bitwise_and(partner_mask, 1), jnp.bitwise_and(me, 1).reshape(1), edge_count, own_t, part_t, part_there,
       rel_here.reshape(half, width), rel_there.reshape(half, width),
@@ -259,7 +261,7 @@
     part_core = swap(part_grad, 1)
     own_grad = pl.pallas_call(
         last_kernel, out_shape=sh((width, rows), F32), in_specs=[sm] + [vm] * 2, out_specs=vm, name="last",
-        compiler_params=pltpu.CompilerParams(vmem_limit_bytes=16 << 20),
+        compiler_params=pltpu.CompilerParams(vmem_limit_bytes=58 << 20),
     )(edge_count, to_source, source_rows.reshape(lines))
     returned = jnp.where(odd, part_core, part_grad)
     grad_sum = (grad_here.reshape(by_z).astype(F32) + from_core.astype(F32)).astype(BF)

time: 154 us -> 154 us (level)
  Pallas kernels: 33.4 us -> 35.7 us
  other arithmetic: 9.47 us -> 7.27 us
    pallas_call x1, Pallas kernels: 1.69 us -> 4.3 us  [local(): pl.pallas_call(last_kernel, out_shape=sh((width, rows), F32), in_specs=[s...]
  transfers between devices with their start and end apart: 12 -> 12, of which waited for: 7 -> 6; matrix products, arithmetic and copies ran while one was open for 3% -> 3% of each run, Pallas kernels for 1% -> 3%
where the time goes in v3:
time: 154 us; the launch traced here: 153 us
  waiting for transfers between devices  63.7 us (41%)
  starting transfers between devices  40.7 us (26%)
  Pallas kernels  35.7 us (23%)
  other arithmetic  7.27 us (5%)
  local copies, waits for them, and re-layouts  3.62 us (2%)
  between operations  2.08 us (1%)
    ppermute x8, waiting for transfers between devices, swap(): return lax.ppermute(value, 'dom', pairs)  63.6 us
    pallas_call x1, Pallas kernels, local(): pl.pallas_call(train_kernel, out_shape=(sh((width, rows), BF), sh((width,...  31.4 us
    all_to_all x4, starting transfers between devices, exchange(): lax.all_to_all(blocks, 'dom', 0, 0, axis_index_groups=groups_of(shift, bi...  27.7 us
    ppermute x8, starting transfers between devices, swap(): return lax.ppermute(value, 'dom', pairs)  13 us
    pallas_call x1, Pallas kernels, local(): pl.pallas_call(last_kernel, out_shape=sh((width, rows), F32), in_specs=[s...  4.3 us
  transfers between devices with their start and end apart: 12, of which 6 were waited for; matrix products, arithmetic and copies ran while one was open for 3% of the time, Pallas kernels for 3%

profile of v3, /device:TPU:2, one launch (start us, length us, event | category | flops | bytes accessed | tf_op | source)
XLA Modules:
  0.0 153.4 jit_solution(14546886276195030854)
XLA Ops:
  0.6 0.7 convert_element_type.61
  1.4 0.6 broadcast_in_dim.4
  2.0 8.5 %all-to-all-start = ((bf16[8,8,400]{2,1,0:T(8,128)(2,1)}), bf16[8,8,400]{2,1,0:T(8,128)(2,1)S(1)}, u32[]{:S(2)}, u32[]{:S(2)}) async-start(bf16[8,8,400]{2,1,0:T(8,128)(2,1)} %broadcast_in_dim.4), calls=%async_computation | async-start | bytes 131072 | tf_op jit(solution)/shard_map/all_to_all | solution.py:184
  10.5 1.2 convert_bitcast_fusion.bt_in
  12.3 15.1 %conditional.4 = (bf16[400,512]{1,0:T(8,128)(2,1)}) conditional(s32[]{:T(128)} %bitcast.3, bf16[400,512]{1,0:T(8,128)(2,1)S(1)} %convert_bitcast_fusion.bt_in, bf16[400,512]{1,0:T(8,128)(2,1)S(1)} %convert_bitcast_fusion.bt_in, bf16[400,512]{1,0:T(8,128)(2,1)S(1)} %convert_bitcast_fusion.bt_in, ...), branch_computations={%region_0.0_spmd, %region_1.0_spmd, %region_2.0_spmd, %region_3.0_... | conditional | bytes 1638448 | solution.py:192
  12.3 4.8 %collective-permute-start.9 = (bf16[400,512]{1,0:T(8,128)(2,1)S(1)}, bf16[400,512]{1,0:T(8,128)(2,1)}, u32[]{:S(2)}, u32[]{:S(2)}) collective-permute-start(bf16[400,512]{1,0:T(8,128)(2,1)S(1)} %param.10), channel_id=1, source_target_pairs={{0,160},{1,161},{2,162},{3,163},{4,164},{5,165},{6,166},{7,167},{8... | collective-permute-start | bytes 1228808 | tf_op jit(solution)/shard_map/cond/branch_10_fun/ppermute | solution.py:174
  17.2 10.2 %collective-permute-done.9 = bf16[400,512]{1,0:T(8,128)(2,1)} collective-permute-done((bf16[400,512]{1,0:T(8,128)(2,1)S(1)}, bf16[400,512]{1,0:T(8,128)(2,1)}, u32[]{:S(2)}, u32[]{:S(2)}) %collective-permute-start.9) | collective-permute-done | bytes 409632 | tf_op jit(solution)/shard_map/cond/branch_10_fun/ppermute | solution.py:174
  27.4 1.1 broadcast_in_dim.5
  28.5 7.5 %all-to-all-start.1 = ((bf16[16,64,400]{2,1,0:T(8,128)(2,1)}), bf16[16,64,400]{2,1,0:T(8,128)(2,1)S(1)}, u32[]{:S(2)}, u32[]{:S(2)}) async-start(bf16[16,64,400]{2,1,0:T(8,128)(2,1)} %broadcast_in_dim.5), calls=%async_computation.1 | async-start | bytes 2097152 | tf_op jit(solution)/shard_map/all_to_all | solution.py:184
  36.0 20.3 %conditional.5 = (bf16[400,512]{1,0:T(8,128)(2,1)}) conditional(s32[]{:T(128)} %bitcast.4, bf16[400,512]{1,0:T(8,128)(2,1)} %get-tuple-element.136, bf16[400,512]{1,0:T(8,128)(2,1)} %get-tuple-element.136, bf16[400,512]{1,0:T(8,128)(2,1)} %get-tuple-element.136, bf16[400,512]{1,0:T(8,128)(2,1)} %get-tuple-element.136, ...), branch_computations={%region_16.0_spmd, %region_17.0_spmd, %region_18.0_spmd, %region_1... | conditional | bytes 2457648 | solution.py:192
  36.1 2.7 %collective-permute-start.16 = (bf16[400,512]{1,0:T(8,128)(2,1)}, bf16[400,512]{1,0:T(8,128)(2,1)S(1)}, u32[]{:S(2)}, u32[]{:S(2)}) collective-permute-start(bf16[400,512]{1,0:T(8,128)(2,1)} %param.18), channel_id=1, source_target_pairs={{0,4},{1,5},{2,6},{3,7},{4,0},{5,1},{6,2},{7,3},{8,12},{9,13},{10,... | collective-permute-start | bytes 1228808 | tf_op jit(solution)/shard_map/cond/branch_2_fun/ppermute | solution.py:174
  38.8 16.8 %collective-permute-done.16 = bf16[400,512]{1,0:T(8,128)(2,1)S(1)} collective-permute-done((bf16[400,512]{1,0:T(8,128)(2,1)}, bf16[400,512]{1,0:T(8,128)(2,1)S(1)}, u32[]{:S(2)}, u32[]{:S(2)}) %collective-permute-start.16) | collective-permute-done | bytes 409632 | tf_op jit(solution)/shard_map/cond/branch_2_fun/ppermute | solution.py:174
  55.5 0.8 copy.32
  56.3 0.5 collective-permute-start.44
  57.5 2.1 %collective-permute-done.44.pb_in = bf16[400,512]{1,0:T(8,128)(2,1)S(1)} collective-permute-done((bf16[400,512]{1,0:T(8,128)(2,1)}, bf16[400,512]{1,0:T(8,128)(2,1)S(1)}, u32[]{:S(2)}, u32[]{:S(2)}) %collective-permute-start.44) | collective-permute-done | bytes 409632 | tf_op jit(solution)/shard_map/ppermute | solution.py:174
  59.6 1.0 copy-done.6
  60.6 31.4 %train.1 = (bf16[400,512]{1,0:T(8,128)(2,1)S(1)}, bf16[400,3072]{1,0:T(8,128)(2,1)}, bf16[1024,400]{1,0:T(8,128)(2,1)S(1)}, bf16[1024,400]{1,0:T(8,128)(2,1)S(1)}) custom-call(s32[1]{0:T(128)S(6)} %and.19.odd_ref, s32[1]{0:T(128)} %bitcast.core_ref, s32[1]{0:T(128)S(6)} %copy.63.count_ref, bf16[400,512]{1,0:T(8,128)(2,1)S(1)} %convert_bitcast_fusion.bt_in, ...), custom_call_target="tpu_custom_call" | custom-call | tf_op jit(solution)/shard_map/train/pallas_call | solution.py:240
  92.2 2.5 %collective-permute-done.46 = bf16[16,64,400]{2,1,0:T(8,128)(2,1)S(1)} collective-permute-done((bf16[16,64,400]{2,1,0:T(8,128)(2,1)S(1)}, bf16[16,64,400]{2,1,0:T(8,128)(2,1)S(1)}, u32[]{:S(2)}, u32[]{:S(2)}) %collective-permute-start.46) | collective-permute-done | bytes 819232 | tf_op jit(solution)/shard_map/ppermute | solution.py:174
  94.7 1.3 fusion
  96.1 7.2 %all-to-all-start.2 = ((bf16[16,64,400]{2,1,0:T(8,128)(2,1)}), bf16[16,64,400]{2,1,0:T(8,128)(2,1)S(1)}, u32[]{:S(2)}, u32[]{:S(2)}) async-start(bf16[16,64,400]{2,1,0:T(8,128)(2,1)} %fusion), calls=%async_computation.2 | async-start | bytes 2097152 | tf_op jit(solution)/shard_map/all_to_all | solution.py:184
  103.3 4.3 %last.1 = f32[400,512]{1,0:T(8,128)} custom-call(s32[1]{0:T(128)S(6)} %copy.63.count_ref, bf16[400,3072]{1,0:T(8,128)(2,1)} %get-tuple-element.128.xo_ref, s32[24,128]{1,0:T(8,128)} %bitcast.20), custom_call_target="tpu_custom_call" | custom-call | tf_op jit(solution)/shard_map/last/pallas_call | solution.py:262
  107.6 21.9 %conditional.6 = (bf16[400,512]{1,0:T(8,128)(2,1)S(1)}) conditional(s32[]{:T(128)} %bitcast.4, bf16[400,512]{1,0:T(8,128)(2,1)S(1)} %broadcast_select_fusion, bf16[400,512]{1,0:T(8,128)(2,1)S(1)} %broadcast_select_fusion, bf16[400,512]{1,0:T(8,128)(2,1)S(1)} %broadcast_select_fusion, ...), branch_computations={%region_25.26_spmd, %region_26.27_spmd, %region_27.28_spmd, %regio... | conditional | bytes 2457648 | solution.py:192
  107.8 21.5 %collective-permute-done.23 = bf16[400,512]{1,0:T(8,128)(2,1)S(1)} collective-permute-done((bf16[400,512]{1,0:T(8,128)(2,1)S(1)}, bf16[400,512]{1,0:T(8,128)(2,1)S(1)}, u32[]{:S(2)}, u32[]{:S(2)}) %collective-permute-start.23) | collective-permute-done | bytes 409632 | tf_op jit(solution)/shard_map/cond/branch_2_fun/ppermute | solution.py:174
  129.6 0.8 reduce_sum.39
  130.3 4.6 %all-to-all-start.3 = ((bf16[8,8,400]{2,1,0:T(8,128)(2,1)}), bf16[8,8,400]{2,1,0:T(8,128)(2,1)S(1)}, u32[]{:S(2)}, u32[]{:S(2)}) async-start(bf16[8,8,400]{2,1,0:T(8,128)(2,1)} %bitcast.14), calls=%async_computation.3 | async-start | bytes 131072 | tf_op jit(solution)/shard_map/all_to_all | solution.py:184
  134.9 15.2 %conditional.7 = (bf16[400,512]{1,0:T(8,128)(2,1)S(1)}) conditional(s32[]{:T(128)} %bitcast.3, bf16[400,512]{1,0:T(8,128)(2,1)S(1)} %get-tuple-element.138, bf16[400,512]{1,0:T(8,128)(2,1)S(1)} %get-tuple-element.138, bf16[400,512]{1,0:T(8,128)(2,1)S(1)} %get-tuple-element.138, ...), branch_computations={%region_33.34_spmd, %region_34.35_spmd, %region_35.36_spmd, %regio... | conditional | bytes 2457648 | solution.py:192
  135.0 4.6 %collective-permute-start.38 = (bf16[400,512]{1,0:T(8,128)(2,1)S(1)}, bf16[400,512]{1,0:T(8,128)(2,1)S(1)}, u32[]{:S(2)}, u32[]{:S(2)}) collective-permute-start(bf16[400,512]{1,0:T(8,128)(2,1)S(1)} %param.42), channel_id=1, source_target_pairs={{0,160},{1,161},{2,162},{3,163},{4,164},{5,165},{6,166},{7,167},{8... | collective-permute-start | bytes 1228808 | tf_op jit(solution)/shard_map/cond/branch_10_fun/ppermute | solution.py:174
  139.6 10.6 %collective-permute-done.38 = bf16[400,512]{1,0:T(8,128)(2,1)S(1)} collective-permute-done((bf16[400,512]{1,0:T(8,128)(2,1)S(1)}, bf16[400,512]{1,0:T(8,128)(2,1)S(1)}, u32[]{:S(2)}, u32[]{:S(2)}) %collective-permute-start.38) | collective-permute-done | bytes 409632 | tf_op jit(solution)/shard_map/cond/branch_10_fun/ppermute | solution.py:174
  150.4 0.6 fusion.2
  151.0 1.1 bitcast_subtract_fusion
  152.2 0.5 fusion.1
  152.7 0.7 divide_subtract_fusion
  (35 shorter events, 0.8 us)
Async XLA Ops:
  2.0 25.4 %all-to-all-start = ((bf16[8,8,400]{2,1,0:T(8,128)(2,1)}), bf16[8,8,400]{2,1,0:T(8,128)(2,1)S(1)}, u32[]{:S(2)}, u32[]{:S(2)}) async-start(bf16[8,8,400]{2,1,0:T(8,128)(2,1)} %broadcast_in_dim.4), calls=%async_computation | async-start | bytes 131072 | tf_op jit(solution)/shard_map/all_to_all | solution.py:184
  12.3 15.0 %collective-permute-start.9 = (bf16[400,512]{1,0:T(8,128)(2,1)S(1)}, bf16[400,512]{1,0:T(8,128)(2,1)}, u32[]{:S(2)}, u32[]{:S(2)}) collective-permute-start(bf16[400,512]{1,0:T(8,128)(2,1)S(1)} %param.10), channel_id=1, source_target_pairs={{0,160},{1,161},{2,162},{3,163},{4,164},{5,165},{6,166},{7,167},{8... | collective-permute-start | bytes 1228808 | tf_op jit(solution)/shard_map/cond/branch_10_fun/ppermute | solution.py:174
  28.5 27.8 %all-to-all-start.1 = ((bf16[16,64,400]{2,1,0:T(8,128)(2,1)}), bf16[16,64,400]{2,1,0:T(8,128)(2,1)S(1)}, u32[]{:S(2)}, u32[]{:S(2)}) async-start(bf16[16,64,400]{2,1,0:T(8,128)(2,1)} %broadcast_in_dim.5), calls=%async_computation.1 | async-start | bytes 2097152 | tf_op jit(solution)/shard_map/all_to_all | solution.py:184
  36.0 24.6 %copy-start = (s32[3072]{0:T(1024)S(1)}, s32[3072]{0:T(1024)}, u32[]{:S(2)}) copy-start(s32[3072]{0:T(1024)} %param.63) | copy-start | bytes 36868
  36.0 24.6 %copy-start.1 = (s32[12,512]{1,0:T(8,128)S(1)}, s32[12,512]{1,0:T(8,128)}, u32[]{:S(2)}) copy-start(s32[12,512]{1,0:T(8,128)} %n_in.1) | copy-start | bytes 73732
  36.0 24.6 %copy-start.2 = (s32[3072]{0:T(1024)S(1)}, s32[3072]{0:T(1024)}, u32[]{:S(2)}) copy-start(s32[3072]{0:T(1024)} %param.64) | copy-start | bytes 36868
  36.0 24.5 %copy-start.3 = (s32[3072]{0:T(1024)S(1)}, s32[3072]{0:T(1024)}, u32[]{:S(2)}) copy-start(s32[3072]{0:T(1024)} %param.65) | copy-start | bytes 36868
  36.1 19.5 %collective-permute-start.16 = (bf16[400,512]{1,0:T(8,128)(2,1)}, bf16[400,512]{1,0:T(8,128)(2,1)S(1)}, u32[]{:S(2)}, u32[]{:S(2)}) collective-permute-start(bf16[400,512]{1,0:T(8,128)(2,1)} %param.18), channel_id=1, source_target_pairs={{0,4},{1,5},{2,6},{3,7},{4,0},{5,1},{6,2},{7,3},{8,12},{9,13},{10,... | collective-permute-start | bytes 1228808 | tf_op jit(solution)/shard_map/cond/branch_2_fun/ppermute | solution.py:174
  56.3 3.2 %collective-permute-start.45 = (bf16[16,64,400]{2,1,0:T(8,128)(2,1)S(1)}, bf16[16,64,400]{2,1,0:T(8,128)(2,1)S(1)}, u32[]{:S(2)}, u32[]{:S(2)}) collective-permute-start(bf16[16,64,400]{2,1,0:T(8,128)(2,1)S(1)} %all-to-all-done.1), channel_id=1, source_target_pairs={{0,1},{1,0},{2,3},{3,2},{4,5},{5,4},{6,7},{7,6},{8,9},{9,8},{10,11... | collective-permute-start | bytes 2457608 | tf_op jit(solution)/shard_map/ppermute | solution.py:174
  56.3 3.2 %collective-permute-start.44 = (bf16[400,512]{1,0:T(8,128)(2,1)}, bf16[400,512]{1,0:T(8,128)(2,1)S(1)}, u32[]{:S(2)}, u32[]{:S(2)}) collective-permute-start(bf16[400,512]{1,0:T(8,128)(2,1)} %get-tuple-element.137.pa_in), channel_id=1, source_target_pairs={{0,1},{1,0},{2,3},{3,2},{4,5},{5,4},{6,7},{7,6},{8,9},{9,8},{10,11... | collective-permute-start | bytes 1228808 | tf_op jit(solution)/shard_map/ppermute | solution.py:174
  59.6 1.0 copy-start.6
  92.0 2.7 %collective-permute-start.46 = (bf16[16,64,400]{2,1,0:T(8,128)(2,1)S(1)}, bf16[16,64,400]{2,1,0:T(8,128)(2,1)S(1)}, u32[]{:S(2)}, u32[]{:S(2)}) collective-permute-start(bf16[16,64,400]{2,1,0:T(8,128)(2,1)S(1)} %bitcast.24), channel_id=1, source_target_pairs={{0,1},{1,0},{2,3},{3,2},{4,5},{5,4},{6,7},{7,6},{8,9},{9,8},{10,11... | collective-permute-start | bytes 2457608 | tf_op jit(solution)/shard_map/ppermute | solution.py:174
  96.1 33.5 %all-to-all-start.2 = ((bf16[16,64,400]{2,1,0:T(8,128)(2,1)}), bf16[16,64,400]{2,1,0:T(8,128)(2,1)S(1)}, u32[]{:S(2)}, u32[]{:S(2)}) async-start(bf16[16,64,400]{2,1,0:T(8,128)(2,1)} %fusion), calls=%async_computation.2 | async-start | bytes 2097152 | tf_op jit(solution)/shard_map/all_to_all | solution.py:184
  103.3 4.3 %collective-permute-start.47 = (bf16[400,512]{1,0:T(8,128)(2,1)S(1)}, bf16[400,512]{1,0:T(8,128)(2,1)S(1)}, u32[]{:S(2)}, u32[]{:S(2)}) collective-permute-start(bf16[400,512]{1,0:T(8,128)(2,1)S(1)} %get-tuple-element.127), channel_id=1, source_target_pairs={{0,1},{1,0},{2,3},{3,2},{4,5},{5,4},{6,7},{7,6},{8,9},{9,8},{10,11... | collective-permute-start | bytes 1228808 | tf_op jit(solution)/shard_map/ppermute | solution.py:174
  107.7 21.6 %collective-permute-start.23 = (bf16[400,512]{1,0:T(8,128)(2,1)S(1)}, bf16[400,512]{1,0:T(8,128)(2,1)S(1)}, u32[]{:S(2)}, u32[]{:S(2)}) collective-permute-start(bf16[400,512]{1,0:T(8,128)(2,1)S(1)} %param.26), channel_id=1, source_target_pairs={{0,4},{1,5},{2,6},{3,7},{4,0},{5,1},{6,2},{7,3},{8,12},{9,13},{10,... | collective-permute-start | bytes 1228808 | tf_op jit(solution)/shard_map/cond/branch_2_fun/ppermute | solution.py:174
  130.3 21.7 %all-to-all-start.3 = ((bf16[8,8,400]{2,1,0:T(8,128)(2,1)}), bf16[8,8,400]{2,1,0:T(8,128)(2,1)S(1)}, u32[]{:S(2)}, u32[]{:S(2)}) async-start(bf16[8,8,400]{2,1,0:T(8,128)(2,1)} %bitcast.14), calls=%async_computation.3 | async-start | bytes 131072 | tf_op jit(solution)/shard_map/all_to_all | solution.py:184
  134.9 15.3 %copy-start.4 = (f32[400,512]{1,0:T(8,128)S(1)}, f32[400,512]{1,0:T(8,128)}, u32[]{:S(2)}) copy-start(f32[400,512]{1,0:T(8,128)} %last.1) | copy-start | bytes 2457604
  134.9 15.5 %copy-start.8 = (f32[512]{0:T(512)S(1)}, f32[512]{0:T(512)}, u32[]{:S(2)}) copy-start(f32[512]{0:T(512)} %param.59) | copy-start | bytes 6148
  134.9 16.0 %copy-start.5 = (f32[512,400]{0,1:T(8,128)S(1)}, f32[512,400]{0,1:T(8,128)}, u32[]{:S(2)}) copy-start(f32[512,400]{0,1:T(8,128)} %param.58) | copy-start | bytes 2457604
  135.0 15.2 %collective-permute-start.38 = (bf16[400,512]{1,0:T(8,128)(2,1)S(1)}, bf16[400,512]{1,0:T(8,128)(2,1)S(1)}, u32[]{:S(2)}, u32[]{:S(2)}) collective-permute-start(bf16[400,512]{1,0:T(8,128)(2,1)S(1)} %param.42), channel_id=1, source_target_pairs={{0,160},{1,161},{2,162},{3,163},{4,164},{5,165},{6,166},{7,167},{8... | collective-permute-start | bytes 1228808 | tf_op jit(solution)/shard_map/cond/branch_10_fun/ppermute | solution.py:174
  150.2 2.0 %copy-start.9 = (f32[8]{0:T(128)S(1)}, f32[8]{0:T(128)}, u32[]{:S(2)}) copy-start(f32[8]{0:T(128)} %param.61) | copy-start | bytes 100
  150.2 2.5 %copy-start.7 = (f32[8,400]{1,0:T(8,128)S(1)}, f32[8,400]{1,0:T(8,128)}, u32[]{:S(2)}) copy-start(f32[8,400]{1,0:T(8,128)} %param.60) | copy-start | bytes 38404
